TPU v7x, 32 devices: a whole 2x2x4 slice. The times are simulated.
32 devices in a mesh: expert: 16 (over z, y, x), dp: 2 (over core).
Axes of the slice: x: 2, y: 2, z: 4, core: 2. Of those that a mesh axis runs over, the one named last changes fastest.
Arguments:
- tokens: bfloat16 [768, 2048], P(('expert', 'dp')), may hold values from -6 to 6
- cotangent: bfloat16 [768, 2048], P(('expert', 'dp')), may hold values from -6 to 6
- route_gates: bfloat16 [768, 6], P(('expert', 'dp')), may hold values from 0.049804688 to 1
- routes: int32 [768, 6], P(('expert', 'dp')), may hold values from 0 to 15, all different within a row; in each aligned block of 24 rows (0 to 23, 24 to 47, ...) at most 12 rows name the same one
- w_gate: bfloat16 [16, 1408, 2048], P('expert', 'dp'), may hold values from -0.125 to 0.125
- w_up: bfloat16 [16, 1408, 2048], P('expert', 'dp'), may hold values from -0.125 to 0.125
- w_down: bfloat16 [16, 1408, 2048], P('expert', 'dp'), may hold values from -0.15625 to 0.15625
Outputs:
- layer_out: bfloat16 [768, 2048], P(('expert', 'dp'))
- token_grad: bfloat16 [768, 2048], P(('expert', 'dp'))
- gate_grad: float32 [768, 6], P(('expert', 'dp'))
- grad_gate_proj: float32 [16, 1408, 2048], P('expert', 'dp')
- grad_up_proj: float32 [16, 1408, 2048], P('expert', 'dp')
- grad_down_proj: float32 [16, 1408, 2048], P('expert', 'dp')
Inputs may be any that keep to these rules, and one draw needn't show every extreme that they name: `routes`: each row names 6 different experts. In the rows of one device no expert is named by more than 12 rows.
All inputs are finite; a program needn't handle non-finite values.
Results may differ from a plain program's by a relative error of at most 0.01.
Values may be sent and summed in bfloat16 or wider, within the bound.
A program may use at most 128 MiB of HBM per device.

v0:
```python
import jax
import jax.numpy as jnp
from jax import lax
from jax.sharding import PartitionSpec as P


def slot_table(route_block, experts, capacity):
    flat_routes = route_block.reshape(-1)
    onehot = (flat_routes[:, None] == jnp.arange(experts, dtype=jnp.int32)[None, :]).astype(
        jnp.int32
    )
    before = jnp.cumsum(onehot, axis=0) - onehot
    slot_rank = jnp.sum(before * onehot, axis=1)
    slot_index = flat_routes * capacity + slot_rank
    slot_ids = jnp.arange(experts * capacity, dtype=jnp.int32)
    return (slot_ids[:, None] == slot_index[None, :]).astype(jnp.bfloat16)


def prepare(tokens, cotangent, route_gates, route_table):
    token_count, top_count = route_gates.shape
    slot_count = route_table.shape[0]
    token_table = jnp.sum(route_table.reshape(slot_count, token_count, top_count), axis=2)
    scaled = (
        route_gates.astype(jnp.float32)[:, :, None] * cotangent.astype(jnp.float32)[:, None, :]
    ).astype(jnp.bfloat16)
    scaled = scaled.reshape(token_count * top_count, tokens.shape[1])
    sent_in = jnp.dot(token_table, tokens, preferred_element_type=jnp.float32).astype(jnp.bfloat16)
    sent_back = jnp.dot(route_table, scaled, preferred_element_type=jnp.float32).astype(
        jnp.bfloat16
    )
    return (sent_in, sent_back)


def pick_rows(route_table, values):
    dims = (((0,), (0,)), ((), ()))
    if values.dtype == jnp.float32:
        return lax.dot_general(
            route_table.astype(jnp.float32),
            values,
            dims,
            precision=lax.Precision.HIGHEST,
            preferred_element_type=jnp.float32,
        )
    return lax.dot_general(route_table, values, dims, preferred_element_type=jnp.float32)


def combine(route_table, back_out, back_grad, route_gates, cotangent):
    token_count, top_count = route_gates.shape
    route_out = pick_rows(route_table, back_out).reshape(token_count, top_count, -1)
    mixed = jnp.sum(route_gates.astype(jnp.float32)[:, :, None] * route_out, axis=1)
    gate_grad = jnp.sum(cotangent.astype(jnp.float32)[:, None, :] * route_out, axis=2)
    token_grad = jnp.sum(
        pick_rows(route_table, back_grad).reshape(token_count, top_count, -1), axis=1
    )
    return (mixed, token_grad, gate_grad)


def expert_work(rows_in, rows_back, gate_shard, up_shard, down_shard):
    inner = (((1,), (1,)), ((), ()))
    outer = (((0,), (0,)), ((), ()))
    gate_pre = lax.dot_general(rows_in, gate_shard, inner, preferred_element_type=jnp.float32)
    up_pre = lax.dot_general(rows_in, up_shard, inner, preferred_element_type=jnp.float32)
    sigmoid_gate = jax.nn.sigmoid(gate_pre)
    hidden = (gate_pre * sigmoid_gate * up_pre).astype(jnp.bfloat16)
    out_part = jnp.dot(hidden, down_shard, preferred_element_type=jnp.float32).astype(jnp.bfloat16)
    back_hidden = lax.dot_general(rows_back, down_shard, inner, preferred_element_type=jnp.float32)
    grad_pre = (
        back_hidden * up_pre * sigmoid_gate * (1.0 + gate_pre * (1.0 - sigmoid_gate))
    ).astype(jnp.bfloat16)
    grad_upv = (back_hidden * gate_pre * sigmoid_gate).astype(jnp.bfloat16)
    grad_down = lax.dot_general(hidden, rows_back, outer, preferred_element_type=jnp.float32)
    grad_gate = lax.dot_general(grad_pre, rows_in, outer, preferred_element_type=jnp.float32)
    grad_up = lax.dot_general(grad_upv, rows_in, outer, preferred_element_type=jnp.float32)
    back_part = jnp.dot(grad_pre, gate_shard, preferred_element_type=jnp.float32)
    back_part = (
        back_part + jnp.dot(grad_upv, up_shard, preferred_element_type=jnp.float32)
    ).astype(jnp.bfloat16)
    return (out_part, back_part, grad_gate, grad_up, grad_down)


def per_device(tokens, cotangent, route_gates, routes, w_gate, w_up, w_down):
    group_count = lax.axis_size("dp")
    experts = lax.axis_size("expert")
    token_count, top_count = routes.shape
    model_width = tokens.shape[1]
    capacity = max(2, token_count * top_count * 4 // (3 * experts))
    slot_count = experts * capacity
    gate_shard, up_shard, down_shard = (w_gate[0], w_up[0], w_down[0])
    route_table = slot_table(routes, experts, capacity)
    sent_in, sent_back = prepare(tokens, cotangent, route_gates, route_table)
    slot_shape = (experts, capacity, model_width)
    got_in, got_back = (
        lax.all_to_all(
            sent_in.reshape(slot_shape), "expert", split_axis=0, concat_axis=0, tiled=True
        ),
        lax.all_to_all(
            sent_back.reshape(slot_shape), "expert", split_axis=0, concat_axis=0, tiled=True
        ),
    )
    all_in, all_back = (
        lax.all_gather(got_in[None], "dp", axis=0, tiled=True),
        lax.all_gather(got_back[None], "dp", axis=0, tiled=True),
    )
    out_part, back_part, grad_gate, grad_up, grad_down = expert_work(
        all_in.reshape(-1, model_width),
        all_back.reshape(-1, model_width),
        gate_shard,
        up_shard,
        down_shard,
    )
    part_shape = (group_count, slot_count, model_width)
    sum_out, sum_back = (
        lax.psum_scatter(
            out_part.reshape(part_shape), "dp", scatter_dimension=0, tiled=True
        ).astype(jnp.float32),
        lax.psum_scatter(
            back_part.reshape(part_shape), "dp", scatter_dimension=0, tiled=True
        ).astype(jnp.float32),
    )
    ret_out, ret_back = (
        lax.all_to_all(
            sum_out[0].reshape(slot_shape).astype(jnp.bfloat16),
            "expert",
            split_axis=0,
            concat_axis=0,
            tiled=True,
        ).astype(jnp.float32),
        lax.all_to_all(
            sum_back[0].reshape(slot_shape).astype(jnp.bfloat16),
            "expert",
            split_axis=0,
            concat_axis=0,
            tiled=True,
        ).astype(jnp.float32),
    )
    mixed, token_grad, gate_grad = combine(
        route_table,
        ret_out.reshape(slot_count, model_width),
        ret_back.reshape(slot_count, model_width),
        route_gates,
        cotangent,
    )
    return (
        mixed.astype(jnp.bfloat16),
        token_grad.astype(jnp.bfloat16),
        gate_grad,
        grad_gate[None],
        grad_up[None],
        grad_down[None],
    )


def solution(mesh):
    placed = (
        P(("expert", "dp"), None),
        P(("expert", "dp"), None),
        P(("expert", "dp"), None),
        P(("expert", "dp"), None),
        P("expert", "dp", None),
        P("expert", "dp", None),
        P("expert", "dp", None),
    )
    return jax.shard_map(
        per_device,
        mesh=mesh,
        in_specs=placed,
        out_specs=(
            P(("expert", "dp"), None),
            P(("expert", "dp"), None),
            P(("expert", "dp"), None),
            P("expert", "dp", None),
            P("expert", "dp", None),
            P("expert", "dp", None),
        ),
        check_vma=False,
    )
```

profile of v0, /device:TPU:8, one launch (start us, length us, event | category | flops | bytes accessed | tf_op | source)
XLA Modules:
  0.0 199.8 jit_solution(12785180865042702158)
XLA Ops:
  14.5 7.2 %all-to-all-start = ((bf16[16,12,2048]{2,1,0:T(8,128)(2,1)}), bf16[16,12,2048]{2,1,0:T(8,128)(2,1)}, u32[]{:S(2)}, u32[]{:S(2)}) async-start(bf16[16,12,2048]{2,1,0:T(8,128)(2,1)} %reshape.119), calls=%async_computation | async-start | bytes 2097152 | tf_op jit(solution)/shard_map/all_to_all | solution.py:93
  23.3 2.5 %mul.86 = f32[144,2048]{1,0:T(8,128)} reshape(f32[24,6,2048]{2,1,0:T(8,128)} %mul.85.clone) | data formatting | bytes 2359296 | tf_op jit(solution)/shard_map/mul | solution.py:24
  25.7 21.6 %all-to-all-done = bf16[16,12,2048]{2,1,0:T(8,128)(2,1)} async-done(((bf16[16,12,2048]{2,1,0:T(8,128)(2,1)}), bf16[16,12,2048]{2,1,0:T(8,128)(2,1)}, u32[]{:S(2)}, u32[]{:S(2)}) %all-to-all-start) | async-done | bytes 786464 | tf_op jit(solution)/shard_map/all_to_all | solution.py:93
  47.3 2.5 %copy.51 = bf16[16,12,2048]{2,0,1:T(8,128)(2,1)} copy(bf16[16,12,2048]{2,1,0:T(8,128)(2,1)} %all-to-all-done) | data formatting | bytes 1572864 | tf_op jit(solution)/shard_map/all_to_all | solution.py:93
  49.9 2.6 %convolution_convert_fusion = bf16[192,2048]{1,0:T(8,128)(2,1)} fusion(f32[144,2048]{1,0:T(8,128)} %mul.86, f32[144]{0:T(256)S(1)} %mul.83, s32[144]{0:T(256)S(1)} %multiply_add_fusion.1), kind=kOutput, calls=%fused_computation.17 | convolution fusion | flops 114256896 | bytes 1967232 | tf_op jit(solution)/shard_map/dot_general | solution.py:28
  54.6 29.1 %all_to_all.20 = bf16[16,12,2048]{2,1,0:T(8,128)(2,1)S(1)} all-to-all(bf16[16,12,2048]{2,1,0:T(8,128)(2,1)} %reshape.123), channel_id=1, replica_groups=mesh['expert'=16,'dp'=2] {'expert'}, dimensions={0} | all-to-all | bytes 1572864 | tf_op jit(solution)/shard_map/all_to_all | solution.py:96
  85.3 3.6 %copy.52 = bf16[32,12,2048]{2,1,0:T(8,128)(2,1)} copy(bf16[32,12,2048]{2,0,1:T(8,128)(2,1)} %all-gather.5.cloned.1.call-done) | data formatting | bytes 3145728 | tf_op jit(solution)/shard_map/all_gather | solution.py:101
  88.9 3.7 %reshape.120 = bf16[384,2048]{1,0:T(8,128)(2,1)} reshape(bf16[32,12,2048]{2,1,0:T(8,128)(2,1)} %copy.52) | data formatting | bytes 3145728 | tf_op jit(solution)/shard_map/reshape | solution.py:105
  93.7 3.6 %copy.57 = bf16[32,12,2048]{2,1,0:T(8,128)(2,1)} copy(bf16[32,12,2048]{2,0,1:T(8,128)(2,1)} %all-gather.7.cloned.1.call-done) | data formatting | bytes 3145728 | tf_op jit(solution)/shard_map/all_gather | solution.py:102
  97.4 3.6 %reshape.124 = bf16[384,2048]{1,0:T(8,128)(2,1)} reshape(bf16[32,12,2048]{2,1,0:T(8,128)(2,1)} %copy.57) | data formatting | bytes 3145728 | tf_op jit(solution)/shard_map/reshape | solution.py:106
  101.0 4.1 %fusion.6 = f32[384,704]{0,1:T(8,128)S(1)} fusion(bf16[384,2048]{1,0:T(8,128)(2,1)} %reshape.120, bf16[1,704,2048]{2,1,0:T(8,128)(2,1)} %param.12), kind=kOutput, calls=%fused_computation.10 | convolution fusion | flops 1107296256 | bytes 5537792 | tf_op jit(solution)/shard_map/dot_general | solution.py:62
  106.8 2.9 %multiply_convert_fusion.2 = (bf16[384,704]{0,1:T(8,128)(2,1)S(1)}, bf16[384,704]{0,1:T(8,128)(2,1)}, bf16[384,704]{0,1:T(8,128)(2,1)S(1)}) fusion(f32[384,704]{0,1:T(8,128)S(1)} %fusion, f32[384,704]{0,1:T(8,128)S(1)} %fusion.6, bf16[384,2048]{1,0:T(8,128)(2,1)S(1)} %copy-done.1, bf16[1,704,2048]{2,1,0:T(8,128)(2,1)S(1)} %copy-done), kind=kOutput, calls=%fused_computation.24 | convolution fusion | flops 1111621632 | bytes 8241152 | tf_op jit(solution)/shard_map/dot_general | solution.py:61
  111.2 2.7 %add_convert_fusion = bf16[384,2048]{1,0:T(8,128)(2,1)} fusion(f32[384,2048]{1,0:T(8,128)S(1)} %fusion.4, bf16[384,704]{0,1:T(8,128)(2,1)S(1)} %get-tuple-element.8, bf16[1,704,2048]{2,1,0:T(8,128)(2,1)S(1)} %copy-done), kind=kOutput, calls=%fused_computation.3 | convolution fusion | flops 1108869120 | bytes 8142848 | tf_op jit(solution)/shard_map/dot_general | solution.py:74
  113.9 4.6 %fusion.12 = bf16[384,2048]{1,0:T(8,128)(2,1)} fusion(bf16[384,704]{0,1:T(8,128)(2,1)} %get-tuple-element.9, bf16[1,704,2048]{2,1,0:T(8,128)(2,1)} %param.13), kind=kOutput, calls=%fused_computation.16 | convolution fusion | flops 1108082688 | bytes 4997120 | tf_op jit(solution)/shard_map/dot_general | solution.py:65
  118.5 5.9 %reduce-scatter.5.cloned.1.call-done = bf16[1,192,2048]{2,1,0:T(8,128)(2,1)} async-done(((bf16[2,192,2048]{2,1,0:T(8,128)(2,1)}), bf16[1,192,2048]{2,1,0:T(8,128)(2,1)}) %reduce-scatter.5.cloned.1.call-update) | async-done | bytes 786448 | tf_op jit(solution)/shard_map/reduce_scatter | solution.py:116
  126.5 7.0 %all-to-all-start.3 = ((bf16[16,12,2048]{2,1,0:T(8,128)(2,1)}), bf16[16,12,2048]{2,1,0:T(8,128)(2,1)}, u32[]{:S(2)}, u32[]{:S(2)}) async-start(bf16[16,12,2048]{2,1,0:T(8,128)(2,1)} %convert_element_type.77), calls=%async_computation.5 | async-start | bytes 2097152 | tf_op jit(solution)/shard_map/all_to_all | solution.py:128
  133.5 3.9 %reduce-scatter.3.cloned.1.call-done = bf16[1,192,2048]{2,1,0:T(8,128)(2,1)} async-done(((bf16[2,192,2048]{2,1,0:T(8,128)(2,1)}), bf16[1,192,2048]{2,1,0:T(8,128)(2,1)}) %reduce-scatter.3.cloned.1.call-update) | async-done | bytes 786448 | tf_op jit(solution)/shard_map/reduce_scatter | solution.py:113
  139.5 19.8 %all-to-all-done.3 = bf16[16,12,2048]{2,1,0:T(8,128)(2,1)} async-done(((bf16[16,12,2048]{2,1,0:T(8,128)(2,1)}), bf16[16,12,2048]{2,1,0:T(8,128)(2,1)}, u32[]{:S(2)}, u32[]{:S(2)}) %all-to-all-start.3) | async-done | bytes 786464 | tf_op jit(solution)/shard_map/all_to_all | solution.py:128
  159.4 5.0 %all-to-all-start.1 = ((bf16[16,12,2048]{2,1,0:T(8,128)(2,1)}), bf16[16,12,2048]{2,1,0:T(8,128)(2,1)}, u32[]{:S(2)}, u32[]{:S(2)}) async-start(bf16[16,12,2048]{2,1,0:T(8,128)(2,1)} %convert_element_type.69), calls=%async_computation.2 | async-start | bytes 2097152 | tf_op jit(solution)/shard_map/all_to_all | solution.py:121
  165.3 5.9 %convolution_bitcast_fusion = f32[1,704,2048]{2,1,0:T(8,128)} fusion(bf16[384,704]{0,1:T(8,128)(2,1)} %get-tuple-element.9, bf16[384,2048]{1,0:T(8,128)(2,1)} %reshape.124), kind=kOutput, calls=%fused_computation | convolution fusion | flops 1107296256 | bytes 7880704 | tf_op jit(solution)/shard_map/dot_general | solution.py:71
  171.2 4.2 %convolution_bitcast_fusion.2 = f32[1,704,2048]{2,1,0:T(8,128)} fusion(bf16[384,704]{0,1:T(8,128)(2,1)S(1)} %copy-done.7, bf16[384,2048]{1,0:T(8,128)(2,1)S(1)} %copy-done.2), kind=kOutput, calls=%fused_computation.2 | convolution fusion | flops 1107296256 | bytes 7880704 | tf_op jit(solution)/shard_map/dot_general | solution.py:72
  175.4 4.2 %convolution_bitcast_fusion.1 = f32[1,704,2048]{2,1,0:T(8,128)} fusion(bf16[384,704]{0,1:T(8,128)(2,1)S(1)} %get-tuple-element.10, bf16[384,2048]{1,0:T(8,128)(2,1)S(1)} %copy-done.2), kind=kOutput, calls=%fused_computation.1 | convolution fusion | flops 1107296256 | bytes 7880704 | tf_op jit(solution)/shard_map/dot_general | solution.py:73
  183.8 5.1 %all-to-all-done.1 = bf16[16,12,2048]{2,1,0:T(8,128)(2,1)} async-done(((bf16[16,12,2048]{2,1,0:T(8,128)(2,1)}), bf16[16,12,2048]{2,1,0:T(8,128)(2,1)}, u32[]{:S(2)}, u32[]{:S(2)}) %all-to-all-start.1) | async-done | bytes 786464 | tf_op jit(solution)/shard_map/all_to_all | solution.py:121
  191.0 2.2 %multiply_reduce_fusion = (f32[24,6]{0,1:T(8,128)}, bf16[24,2048]{1,0:T(8,128)(2,1)}) fusion(f32[24,2048]{1,0:T(8,128)S(1)} %copy-done.9, f32[24,6]{0,1:T(8,128)S(1)} %convert_element_type.63, bf16[192,2048,1]{1,0,2:T(8,128)(2,1)} %reshape.132, pred[24,6,192]{2,1,0:T(8,128)(4,1)S(1)} %eq.67), kind=kOutput, calls=%fused_computation.20 | convolution fusion | flops 114376560 | bytes 1110144 | tf_op jit(solution)/shard_map/dot_general | solution.py:37
  (65 shorter events, 28.3 us)
Async XLA Ops:
  7.2 99.6 %copy-start = (bf16[1,704,2048]{2,1,0:T(8,128)(2,1)S(1)}, bf16[1,704,2048]{2,1,0:T(8,128)(2,1)}, u32[]{:S(2)}) copy-start(bf16[1,704,2048]{2,1,0:T(8,128)(2,1)} %param.11) | copy-start | bytes 8650756
  12.3 9.4 %copy-start.10 = (bf16[24,6]{0,1:T(8,128)(2,1)S(1)}, bf16[24,6]{0,1:T(8,128)(2,1)}, u32[]{:S(2)}) copy-start(bf16[24,6]{0,1:T(8,128)(2,1)} %param.9) | copy-start | bytes 868
  12.3 9.6 %copy-start.8 = (bf16[24,2048]{1,0:T(8,128)(2,1)S(1)}, bf16[24,2048]{1,0:T(8,128)(2,1)}, u32[]{:S(2)}) copy-start(bf16[24,2048]{1,0:T(8,128)(2,1)} %param.8) | copy-start | bytes 294916
  14.5 32.9 %all-to-all-start = ((bf16[16,12,2048]{2,1,0:T(8,128)(2,1)}), bf16[16,12,2048]{2,1,0:T(8,128)(2,1)}, u32[]{:S(2)}, u32[]{:S(2)}) async-start(bf16[16,12,2048]{2,1,0:T(8,128)(2,1)} %reshape.119), calls=%async_computation | async-start | bytes 2097152 | tf_op jit(solution)/shard_map/all_to_all | solution.py:93
  21.7 63.6 %all-gather.5.cloned.1.call-start = ((), (), s32[]{:S(2)}) async-start(), calls=%async_computation.8 | async-start | bytes 2359296 | tf_op jit(solution)/shard_map/all_gather | solution.py:101
  49.9 43.9 %all-gather.7.cloned.1.call-start = ((), (), s32[]{:S(2)}) async-start(), calls=%async_computation.9 | async-start | bytes 2359296 | tf_op jit(solution)/shard_map/all_gather | solution.py:102
  85.0 39.3 %reduce-scatter.5.cloned.1.call-start = ((), (), s32[]{:S(2)}) async-start(), calls=%async_computation.7 | async-start | bytes 2359296 | tf_op jit(solution)/shard_map/reduce_scatter | solution.py:116
  101.0 4.1 %copy-start.4 = (bf16[384,2048]{1,0:T(8,128)(2,1)S(1)}, bf16[384,2048]{1,0:T(8,128)(2,1)}, u32[]{:S(2)}) copy-start(bf16[384,2048]{1,0:T(8,128)(2,1)} %reshape.124) | copy-start | bytes 4718596
  101.0 4.1 %copy-start.5 = (bf16[1,704,2048]{2,1,0:T(8,128)(2,1)S(1)}, bf16[1,704,2048]{2,1,0:T(8,128)(2,1)}, u32[]{:S(2)}) copy-start(bf16[1,704,2048]{2,1,0:T(8,128)(2,1)} %param.13) | copy-start | bytes 8650756
  105.1 1.7 copy-start.1
  106.8 2.9 %copy-start.3 = (bf16[1,704,2048]{2,1,0:T(8,128)(2,1)S(1)}, bf16[1,704,2048]{2,1,0:T(8,128)(2,1)}, u32[]{:S(2)}) copy-start(bf16[1,704,2048]{2,1,0:T(8,128)(2,1)} %param.12) | copy-start | bytes 8650756
  109.7 1.4 copy-start.6
  113.9 23.5 %reduce-scatter.3.cloned.1.call-start = ((), (), s32[]{:S(2)}) async-start(), calls=%async_computation.6 | async-start | bytes 2359296 | tf_op jit(solution)/shard_map/reduce_scatter | solution.py:113
  126.5 32.8 %all-to-all-start.3 = ((bf16[16,12,2048]{2,1,0:T(8,128)(2,1)}), bf16[16,12,2048]{2,1,0:T(8,128)(2,1)}, u32[]{:S(2)}, u32[]{:S(2)}) async-start(bf16[16,12,2048]{2,1,0:T(8,128)(2,1)} %convert_element_type.77), calls=%async_computation.5 | async-start | bytes 2097152 | tf_op jit(solution)/shard_map/all_to_all | solution.py:128
  159.4 29.6 %all-to-all-start.1 = ((bf16[16,12,2048]{2,1,0:T(8,128)(2,1)}), bf16[16,12,2048]{2,1,0:T(8,128)(2,1)}, u32[]{:S(2)}, u32[]{:S(2)}) async-start(bf16[16,12,2048]{2,1,0:T(8,128)(2,1)} %convert_element_type.69), calls=%async_computation.2 | async-start | bytes 2097152 | tf_op jit(solution)/shard_map/all_to_all | solution.py:121
  165.3 5.9 %copy-start.2 = (bf16[384,2048]{1,0:T(8,128)(2,1)S(1)}, bf16[384,2048]{1,0:T(8,128)(2,1)}, u32[]{:S(2)}) copy-start(bf16[384,2048]{1,0:T(8,128)(2,1)} %reshape.120) | copy-start | bytes 4718596
  165.3 5.9 %copy-start.7 = (bf16[384,704]{0,1:T(8,128)(2,1)S(1)}, bf16[384,704]{0,1:T(8,128)(2,1)}, u32[]{:S(2)}) copy-start(bf16[384,704]{0,1:T(8,128)(2,1)} %copy-done.6) | copy-start | bytes 1622020
  181.7 9.4 %copy-start.9 = (f32[24,2048]{1,0:T(8,128)S(1)}, f32[24,2048]{1,0:T(8,128)}, u32[]{:S(2)}) copy-start(f32[24,2048]{1,0:T(8,128)} %convert_element_type.71) | copy-start | bytes 589828
Sparse Core Ops, SparseCore 0:
  50.0 8.7 all-gather.4
  85.2 8.5 all-gather.6
  114.0 10.3 reduce-scatter.4
  127.0 10.3 reduce-scatter.2
where the time goes:
time: 201 us; the launch traced here: 200 us
  waiting for transfers between devices  57.5 us (29%)
  matrix products  40.8 us (20%)
  local copies, waits for them, and re-layouts  36.6 us (18%)
  blocking collectives  29.1 us (14%)
  starting transfers between devices  19.6 us (10%)
  between operations  14 us (7%)
  other arithmetic  2.33 us (1%)
    all_to_all x1, blocking collectives, per_device(): lax.all_to_all(sent_back.reshape(slot_shape), 'expert', split_axis=0, con...  29.1 us
    all_to_all x1, waiting for transfers between devices, per_device(): lax.all_to_all(sent_in.reshape(slot_shape), 'expert', split_axis=0, conca...  21.6 us
    all_to_all x1, waiting for transfers between devices, per_device(): lax.all_to_all(sum_back[0].reshape(slot_shape).astype(jnp.bfloat16), 'exp...  19.8 us
    all_to_all x1, starting transfers between devices, per_device(): lax.all_to_all(sent_in.reshape(slot_shape), 'expert', split_axis=0, conca...  7.22 us
    all_to_all x1, starting transfers between devices, per_device(): lax.all_to_all(sum_back[0].reshape(slot_shape).astype(jnp.bfloat16), 'exp...  6.98 us
    dot_general x1, matrix products, expert_work(): lax.dot_general(hidden, rows_back, outer, preferred_element_type=jnp.floa...  5.91 us
    reduce_scatter x1, waiting for transfers between devices, per_device(): lax.psum_scatter(back_part.reshape(part_shape), 'dp', scatter_dimension=0...  5.85 us
    all_to_all x1, waiting for transfers between devices, per_device(): lax.all_to_all(sum_out[0].reshape(slot_shape).astype(jnp.bfloat16), 'expe...  5.09 us
  transfers between devices with their start and end apart: 7, of which 6 were waited for; matrix products, arithmetic and copies ran while one was open for 23% of the time, Pallas kernels for 0%

commit v1 on v0

v1 whole, which is shorter than its diff:
```python
import jax
import jax.numpy as jnp
from jax import lax
from jax.sharding import PartitionSpec as P

AXES = ("expert", "dp")
INNER = (((1,), (1,)), ((), ()))
OUTER = (((0,), (0,)), ((), ()))


def dot_f32(left, right, dims=(((1,), (0,)), ((), ()))):
    return lax.dot_general(left, right, dims, preferred_element_type=jnp.float32)


def per_device(tokens, cotangent, route_gates, routes, w_gate, w_up, w_down):
    experts = lax.axis_size("expert")
    blocks = experts * lax.axis_size("dp")
    token_count, top_count = routes.shape
    capacity = max(2, token_count * top_count * 4 // (3 * experts))
    total = blocks * token_count
    slots = blocks * capacity
    gate_shard, up_shard, down_shard = (w_gate[0], w_up[0], w_down[0])
    me = lax.axis_index("expert")

    routing = jnp.concatenate(
        [routes.astype(jnp.float32), route_gates.astype(jnp.float32)], axis=1
    )
    routing = lax.all_gather(routing, AXES, axis=0, tiled=True)
    all_tokens = lax.all_gather(tokens, AXES, axis=0, tiled=True)
    all_cot = lax.all_gather(cotangent, AXES, axis=0, tiled=True)

    match = (routing[:, :top_count] == me.astype(jnp.float32)).astype(jnp.float32)
    gates = jnp.sum(match * routing[:, top_count:], axis=1)
    used = jnp.sum(match, axis=1)
    used_blocks = used.reshape(blocks, token_count)
    order = jnp.arange(token_count, dtype=jnp.int32)
    lower = (order[:, None] < order[None, :]).astype(jnp.bfloat16)
    rank = dot_f32(used_blocks.astype(jnp.bfloat16), lower)
    base = (jnp.arange(blocks, dtype=jnp.int32) * capacity).astype(jnp.float32)
    slot = jnp.where(used_blocks > 0, rank + base[:, None], -1.0).reshape(total)
    slot_ids = jnp.arange(slots, dtype=jnp.int32).astype(jnp.float32)
    hit = slot_ids[:, None] == slot[None, :]
    pick = hit.astype(jnp.bfloat16)
    weigh = jnp.where(hit, gates[None, :], 0.0).astype(jnp.bfloat16)
    row_gate = jnp.sum(jnp.where(hit, gates[None, :], 0.0), axis=1)

    rows_in = dot_f32(pick, all_tokens).astype(jnp.bfloat16)
    gate_pre = dot_f32(rows_in, gate_shard, INNER)
    up_pre = dot_f32(rows_in, up_shard, INNER)
    sig = jax.nn.sigmoid(gate_pre)
    hidden = (gate_pre * sig * up_pre).astype(jnp.bfloat16)
    out_part = dot_f32(hidden, down_shard).astype(jnp.bfloat16)
    mixed = dot_f32(weigh, out_part, OUTER).astype(jnp.bfloat16)
    mixed = lax.psum_scatter(mixed, AXES, scatter_dimension=0, tiled=True)

    cot_rows = dot_f32(pick, all_cot)
    row_grad = jnp.sum(cot_rows * out_part.astype(jnp.float32), axis=1)
    rows_back = (cot_rows * row_gate[:, None]).astype(jnp.bfloat16)
    token_gg = jnp.sum(jnp.where(hit, row_grad[:, None], 0.0), axis=0)
    gate_grad = lax.psum_scatter(
        match * token_gg[:, None], AXES, scatter_dimension=0, tiled=True
    )
    back_hidden = dot_f32(rows_back, down_shard, INNER)
    grad_pre = (back_hidden * up_pre * sig * (1.0 + gate_pre * (1.0 - sig))).astype(jnp.bfloat16)
    grad_upv = (back_hidden * gate_pre * sig).astype(jnp.bfloat16)
    back_part = (dot_f32(grad_pre, gate_shard) + dot_f32(grad_upv, up_shard)).astype(jnp.bfloat16)
    token_grad = dot_f32(pick, back_part, OUTER).astype(jnp.bfloat16)
    token_grad = lax.psum_scatter(token_grad, AXES, scatter_dimension=0, tiled=True)
    grad_down = dot_f32(hidden, rows_back, OUTER)
    grad_gate = dot_f32(grad_pre, rows_in, OUTER)
    grad_up = dot_f32(grad_upv, rows_in, OUTER)
    return (mixed, token_grad, gate_grad, grad_gate[None], grad_up[None], grad_down[None])


def solution(mesh):
    row = P(("expert", "dp"), None)
    wide = P("expert", "dp", None)
    return jax.shard_map(
        per_device,
        mesh=mesh,
        in_specs=(row, row, row, row, wide, wide, wide),
        out_specs=(row, row, row, wide, wide, wide),
        check_vma=False,
    )
```

time: 201 us -> 354 us (1.76)
  waiting for transfers between devices: 57.5 us -> 213 us
  blocking collectives: 29.1 us -> 75.9 us
  local copies, waits for them, and re-layouts: 36.6 us -> 3.19 us
  starting transfers between devices: 19.6 us -> 0.34 us
    reduce_scatter x2, waiting for transfers between devices: 9.73 us -> 143 us  [the longest x1 107 us: per_device(): lax.psum_scatter(token_grad, AXES, scatter_dimension=0, tiled=True)]
    all_gather x2, waiting for transfers between devices: 1.13 us -> 68.6 us  [the longest x1 45.9 us: per_device(): all_cot = lax.all_gather(cotangent, AXES, axis=0, tiled=True)]
    all_to_all x3 -> x0, waiting for transfers between devices: 46.5 us -> none  [the longest x1 21.6 us: per_device(): lax.all_to_all(sent_in.reshape(slot_shape), 'expert', split_axis=0, conca...]
    unnamed x0 -> x1, blocking collectives: none -> 39.6 us
    all_gather x0 -> x1, blocking collectives: none -> 36.3 us  [per_device(): routing = lax.all_gather(routing, AXES, axis=0, tiled=True)]
    all_to_all x1 -> x0, blocking collectives: 29.1 us -> none  [per_device(): lax.all_to_all(sent_back.reshape(slot_shape), 'expert', split_axis=0, con...]
    all_to_all x3 -> x0, starting transfers between devices: 19.2 us -> none  [the longest x1 7.22 us: per_device(): lax.all_to_all(sent_in.reshape(slot_shape), 'expert', split_axis=0, conca...]
    reshape x7 -> x0, local copies, waits for them, and re-layouts: 15.8 us -> none  [the longest x1 3.72 us: per_device(): all_in.reshape(-1, model_width)]
  transfers between devices with their start and end apart: 7 -> 4, of which waited for: 6 -> 4; matrix products, arithmetic and copies ran while one was open for 23% -> 13% of each run, Pallas kernels for 0% -> 0%
where the time goes in v1:
time: 354 us; the launch traced here: 352 us
  waiting for transfers between devices  213 us (60%)
  blocking collectives  75.9 us (21%)
  matrix products  44.1 us (12%)
  between operations  14 us (4%)
    reduce_scatter x1, waiting for transfers between devices, per_device(): lax.psum_scatter(token_grad, AXES, scatter_dimension=0, tiled=True)  107 us
    all_gather x1, waiting for transfers between devices, per_device(): all_cot = lax.all_gather(cotangent, AXES, axis=0, tiled=True)  45.9 us
    dot_general x13, matrix products, dot_f32(): lax.dot_general(left, right, dims, preferred_element_type=jnp.float32)  44.1 us
    unnamed x1, blocking collectives  39.6 us
    all_gather x1, blocking collectives, per_device(): routing = lax.all_gather(routing, AXES, axis=0, tiled=True)  36.3 us
    reduce_scatter x1, waiting for transfers between devices, per_device(): mixed = lax.psum_scatter(mixed, AXES, scatter_dimension=0, tiled=True)  36.1 us
    all_gather x1, waiting for transfers between devices, per_device(): all_tokens = lax.all_gather(tokens, AXES, axis=0, tiled=True)  22.8 us
  transfers between devices with their start and end apart: 4, of which 4 were waited for; matrix products, arithmetic and copies ran while one was open for 13% of the time, Pallas kernels for 0%

profile of v1, /device:TPU:8, one launch (start us, length us, event | category | flops | bytes accessed | tf_op | source)
XLA Modules:
  0.0 352.3 jit_solution(16330809885407692929)
XLA Ops:
  7.2 0.7 all-gather.4.cloned.1.call-update
  8.0 0.7 all-gather.6.cloned.1.call-update
  8.7 0.7 convert_element_type.69
  9.4 0.7 convert_element_type.68
  10.1 36.3 %all-gather = f32[32,24,12]{1,2,0:T(8,128)S(1)} all-gather(f32[1,24,12]{1,2,0:T(8,128)S(1)} %maximum_bitcast_fusion), channel_id=1, replica_groups=mesh['expert'=16,'dp'=2] {'expert','dp'}, dimensions={0}, use_global_device_ids=true | all-gather | bytes 38016 | tf_op jit(solution)/shard_map/all_gather | solution.py:28
  47.3 22.8 %all-gather.4.cloned.1.call-done = bf16[768,2048]{1,0:T(8,128)(2,1)} async-done(((bf16[24,2048]{1,0:T(8,128)(2,1)}), bf16[768,2048]{1,0:T(8,128)(2,1)}) %all-gather.4.cloned.1.call-update) | async-done | bytes 3145744 | tf_op jit(solution)/shard_map/all_gather | solution.py:29
  70.1 3.3 convolution_convert_fusion.2
  73.4 1.7 fusion.10
  75.1 0.7 copy-done.3
  75.8 2.7 multiply_convert_fusion.3
  78.5 1.4 fusion.12
  80.0 1.1 copy-done.5
  81.1 3.6 %convolution_convert_fusion.1 = bf16[768,2048]{1,0:T(8,128)(2,1)} fusion(bf16[384,2048]{1,0:T(8,128)(2,1)S(1)} %fusion.12, f32[768]{0:T(1024)S(1)} %get-tuple-element.8, f32[768]{0:T(1024)S(1)} %eq.24, f32[384]{0:T(512)S(1)} %iota_convert_fusion), kind=kOutput, calls=%fused_computation.4 | convolution fusion | flops 1210122240 | bytes 4726272 | tf_op jit(solution)/shard_map/dot_general | solution.py:12
  84.9 45.9 %all-gather.6.cloned.1.call-done = bf16[768,2048]{1,0:T(8,128)(2,1)} async-done(((bf16[24,2048]{1,0:T(8,128)(2,1)}), bf16[768,2048]{1,0:T(8,128)(2,1)}) %all-gather.6.cloned.1.call-update) | async-done | bytes 3145744 | tf_op jit(solution)/shard_map/all_gather | solution.py:30
  130.8 4.0 %multiply_reduce_fusion = (f32[384]{0:T(512)S(1)}, f32[384,2048]{1,0:T(8,128)S(1)}) fusion(bf16[384,2048]{1,0:T(8,128)(2,1)} %copy-done.5, bf16[768,2048]{1,0:T(8,128)(2,1)} %all-gather.6.cloned.1.call-done, f32[768]{0:T(1024)S(1)} %eq.24, f32[384]{0:T(512)S(1)} %iota_convert_fusion), kind=kOutput, calls=%fused_computation.5 | convolution fusion | flops 1210613376 | bytes 7870464 | tf_op jit(solution)/shard_map/dot_general | solution.py:12
  135.2 2.8 multiply_convert_fusion.2
  138.1 3.1 fusion.4
  141.2 7.0 %convolution_convert_fusion = bf16[768,2048]{1,0:T(8,128)(2,1)} fusion(f32[384,2048]{1,0:T(8,128)} %fusion.4, bf16[384,704]{0,1:T(8,128)(2,1)} %get-tuple-element.11, bf16[1,704,2048]{2,1,0:T(8,128)(2,1)S(1)} %copy-done, f32[768]{0:T(1024)S(1)} %eq.24, f32[384]{0:T(512)S(1)} %iota_convert_fusion), kind=kOutput, calls=%fused_computation.3 | convolution fusion | flops 2318696448 | bytes 9720320 | tf_op jit(solution)/shard_map/dot_general | solution.py:12
  148.2 39.6 %all-reduce = f32[768,6]{0,1:T(8,128)S(1)} all-reduce(f32[768,6]{0,1:T(8,128)S(1)} %broadcast_select_fusion), channel_id=4, replica_groups=mesh['expert'=16,'dp'=2] {'expert','dp'}, use_global_device_ids=true, to_apply=%region_7.8.clone | all-reduce | flops 4608 | bytes 36864
  188.5 5.9 %convolution_bitcast_fusion.2 = f32[1,704,2048]{2,1,0:T(8,128)} fusion(bf16[384,704]{0,1:T(8,128)(2,1)} %get-tuple-element.11, bf16[384,2048]{1,0:T(8,128)(2,1)} %copy-done.6), kind=kOutput, calls=%fused_computation.2 | convolution fusion | flops 1107296256 | bytes 7880704 | tf_op jit(solution)/shard_map/dot_general | solution.py:12
  194.3 4.2 %convolution_bitcast_fusion.1 = f32[1,704,2048]{2,1,0:T(8,128)} fusion(bf16[384,704]{0,1:T(8,128)(2,1)S(1)} %get-tuple-element.12, bf16[384,2048]{1,0:T(8,128)(2,1)S(1)} %copy-done.7), kind=kOutput, calls=%fused_computation.1 | convolution fusion | flops 1107296256 | bytes 7880704 | tf_op jit(solution)/shard_map/dot_general | solution.py:12
  198.6 4.3 %convolution_bitcast_fusion = f32[1,704,2048]{2,1,0:T(8,128)} fusion(bf16[384,704]{0,1:T(8,128)(2,1)S(1)} %copy-done.9, f32[384,2048]{1,0:T(8,128)S(1)} %copy-done.2, f32[384]{0:T(512)S(1)} %get-tuple-element.7), kind=kOutput, calls=%fused_computation | convolution fusion | flops 1108869120 | bytes 9455104 | tf_op jit(solution)/shard_map/dot_general | solution.py:12
  202.8 36.1 %reduce-scatter.4.cloned.1.call-done = bf16[24,2048]{1,0:T(8,128)(2,1)} async-done(((bf16[768,2048]{1,0:T(8,128)(2,1)}), bf16[24,2048]{1,0:T(8,128)(2,1)}) %reduce-scatter.4.cloned.1.call-update) | async-done | bytes 98320 | tf_op jit(solution)/shard_map/reduce_scatter | solution.py:54
  238.9 106.9 %reduce-scatter.6.cloned.1.call-done = bf16[24,2048]{1,0:T(8,128)(2,1)} async-done(((bf16[768,2048]{1,0:T(8,128)(2,1)}), bf16[24,2048]{1,0:T(8,128)(2,1)}) %reduce-scatter.6.cloned.1.call-update) | async-done | bytes 98320 | tf_op jit(solution)/shard_map/reduce_scatter | solution.py:68
  (51 shorter events, 2.4 us)
Async XLA Ops:
  7.2 66.2 %copy-start = (bf16[1,704,2048]{2,1,0:T(8,128)(2,1)S(1)}, bf16[1,704,2048]{2,1,0:T(8,128)(2,1)}, u32[]{:S(2)}) copy-start(bf16[1,704,2048]{2,1,0:T(8,128)(2,1)} %param.11) | copy-start | bytes 8650756
  7.2 62.9 %all-gather.4.cloned.1.call-start = ((), (), s32[]{:S(2)}) async-start(), calls=%async_computation.2 | async-start | bytes 3244032 | tf_op jit(solution)/shard_map/all_gather | solution.py:29
  7.9 122.9 %all-gather.6.cloned.1.call-start = ((), (), s32[]{:S(2)}) async-start(), calls=%async_computation.4 | async-start | bytes 3244032 | tf_op jit(solution)/shard_map/all_gather | solution.py:30
  8.7 230.2 %reduce-scatter.4.cloned.1.call-start = ((), (), s32[]{:S(2)}) async-start(), calls=%async_computation.3 | async-start | bytes 3244032 | tf_op jit(solution)/shard_map/reduce_scatter | solution.py:54
  73.4 1.7 copy-start.6
  73.4 2.4 copy-start.3
  75.8 2.7 copy-start.12
  75.8 2.7 copy-start.10
  78.5 1.5 copy-start.8
  80.0 1.1 copy-start.5
  84.7 261.1 %reduce-scatter.6.cloned.1.call-start = ((), (), s32[]{:S(2)}) async-start(), calls=%async_computation.5 | async-start | bytes 3244032 | tf_op jit(solution)/shard_map/reduce_scatter | solution.py:68
  130.8 4.4 %copy-start.11 = (bf16[1,704,2048]{2,1,0:T(8,128)(2,1)S(1)}, bf16[1,704,2048]{2,1,0:T(8,128)(2,1)}, u32[]{:S(2)}) copy-start(bf16[1,704,2048]{2,1,0:T(8,128)(2,1)} %param.13) | copy-start | bytes 8650756
  130.8 4.4 %copy-start.13 = (f32[384,704]{0,1:T(8,128)S(1)}, f32[384,704]{0,1:T(8,128)}, u32[]{:S(2)}) copy-start(f32[384,704]{0,1:T(8,128)} %copy-done.12) | copy-start | bytes 3244036
  130.8 4.4 %copy-start.14 = (f32[384,704]{0,1:T(8,128)S(1)}, f32[384,704]{0,1:T(8,128)}, u32[]{:S(2)}) copy-start(f32[384,704]{0,1:T(8,128)} %get-tuple-element.14) | copy-start | bytes 3244036
  134.8 3.2 copy-start.1
  135.2 2.8 copy-start.4
  188.4 5.9 %copy-start.7 = (bf16[384,2048]{1,0:T(8,128)(2,1)S(1)}, bf16[384,2048]{1,0:T(8,128)(2,1)}, u32[]{:S(2)}) copy-start(bf16[384,2048]{1,0:T(8,128)(2,1)} %copy-done.6) | copy-start | bytes 4718596
  194.3 4.2 %copy-start.2 = (f32[384,2048]{1,0:T(8,128)S(1)}, f32[384,2048]{1,0:T(8,128)}, u32[]{:S(2)}) copy-start(f32[384,2048]{1,0:T(8,128)} %copy-done.1) | copy-start | bytes 9437188
  194.3 4.2 %copy-start.9 = (bf16[384,704]{0,1:T(8,128)(2,1)S(1)}, bf16[384,704]{0,1:T(8,128)(2,1)}, u32[]{:S(2)}) copy-start(bf16[384,704]{0,1:T(8,128)(2,1)} %copy-done.8) | copy-start | bytes 1622020
Sparse Core Ops, SparseCore 0:
  10.9 59.1 all-gather.3
  73.0 57.7 all-gather.5
  136.8 102.0 reduce-scatter.3
  244.7 101.0 reduce-scatter.5

commit v2 on v1

v2 whole, which is shorter than its diff:
```python
import functools

import jax
import jax.numpy as jnp
from jax import lax
from jax.experimental import pallas as pl
from jax.experimental.pallas import tpu as pltpu
from jax.sharding import PartitionSpec as P

INNER = (((1,), (1,)), ((), ()))
OUTER = (((0,), (0,)), ((), ()))


def dot_f32(left, right, dims=(((1,), (0,)), ((), ()))):
    return lax.dot_general(left, right, dims, preferred_element_type=jnp.float32)


def gather_kernel(depth, group, *refs):
    ins, outs = refs[:3], refs[3:6]
    own_sem, send_sem, recv_sem = refs[6:]
    me, core = lax.axis_index("expert"), lax.axis_index("dp")
    z, y, x = me // 4, (me // 2) % 2, me % 2

    def at(zz, yy, xx, cc):
        return (zz * 4 + yy * 2 + xx, cc)

    deep = [at((z + k) % depth, y, x, core) for k in range(1, depth)]
    across, beside = at(z, 1 - y, x, core), at(z, y, 1 - x, core)
    mates = [at(z, y, x, (core + k) % group) for k in range(1, group)]
    peers = deep + [across, beside] + mates
    barrier = pltpu.get_barrier_semaphore()
    for peer in peers:
        pl.semaphore_signal(barrier, inc=1, device_id=peer, device_id_type=pl.DeviceIdType.MESH)
    pl.semaphore_wait(barrier, len(peers))

    sent, used = [], [0]

    def push(src, dst, peer):
        index = used[0]
        used[0] += 1
        copy = pltpu.make_async_remote_copy(
            src_ref=src, dst_ref=dst, send_sem=send_sem.at[index], recv_sem=recv_sem.at[index],
            device_id=peer, device_id_type=pl.DeviceIdType.MESH,
        )
        copy.start()
        sent.append(copy)
        return copy

    def arrived(copies):
        for copy in copies:
            copy.wait_recv()

    def share(view):
        return [push(view, view, peer) for peer in mates]

    def pieces(t):
        width = ins[t].shape[1]
        half = width // 2 if width % 256 == 0 else width
        return half, [pl.ds(0, half)] + ([pl.ds(half, width - half)] if half < width else [])

    own = []
    for t in range(3):
        copy = pltpu.make_async_copy(ins[t], outs[t].at[z, y, x, core], own_sem.at[t])
        copy.start()
        own.append(copy)

    def first(t):
        return [push(ins[t], outs[t].at[z, y, x, core], peer) for peer in deep]

    def second(t):
        moved = []
        for i, cols in enumerate(pieces(t)[1]):
            view = outs[t].at[:, y, x, core, :, cols]
            moved.append(push(view, view, across if i == 0 else beside))
        return moved, share(outs[t].at[:, y, x, core])

    def third(t):
        moved, shared = [], []
        for i, cols in enumerate(pieces(t)[1]):
            if i == 0:
                view, new = outs[t].at[:, :, x, core, :, cols], outs[t].at[:, 1 - y, x, core, :, cols]
            else:
                view, new = outs[t].at[:, y, :, core, :, cols], outs[t].at[:, y, 1 - x, core, :, cols]
            moved.append(push(view, view, beside if i == 0 else across))
            shared += share(new)
        return moved, shared

    def last(t):
        shared = []
        for i, cols in enumerate(pieces(t)[1]):
            new = outs[t].at[:, :, 1 - x, core, :, cols] if i == 0 else outs[t].at[:, 1 - y, :, core, :, cols]
            shared += share(new)
        return shared

    pending = []
    step_m, step_a = first(0), first(1)
    for copy in own:
        copy.wait()
    arrived(step_m)
    step_m, shared = second(0)
    pending += shared
    arrived(step_a)
    step_a, shared = second(1)
    pending += shared
    step_b = first(2)
    arrived(step_m)
    step_m, shared = third(0)
    pending += shared
    arrived(step_a)
    step_a, shared = third(1)
    pending += shared
    arrived(step_b)
    step_b, shared = second(2)
    pending += shared
    arrived(step_m)
    pending += last(0)
    arrived(step_a)
    pending += last(1)
    arrived(step_b)
    step_b, shared = third(2)
    pending += shared
    arrived(step_b)
    pending += last(2)
    arrived(pending)
    for copy in sent:
        copy.wait_send()


def gather_all(experts, group, arrays):
    depth = experts // 4
    copies = 3 * (depth + 9 + 5 * group)
    shapes = [
        jax.ShapeDtypeStruct((depth, 2, 2, group) + array.shape, array.dtype) for array in arrays
    ]
    outs = pl.pallas_call(
        functools.partial(gather_kernel, depth, group),
        out_shape=shapes,
        in_specs=[pl.BlockSpec(memory_space=pltpu.VMEM)] * 3,
        out_specs=[pl.BlockSpec(memory_space=pl.ANY)] * 3,
        scratch_shapes=[
            pltpu.SemaphoreType.DMA((3,)),
            pltpu.SemaphoreType.DMA((copies,)),
            pltpu.SemaphoreType.DMA((copies,)),
        ],
        compiler_params=pltpu.CompilerParams(collective_id=0, has_side_effects=True),
    )(*arrays)
    return [out.reshape(-1, out.shape[-1]) for out in outs]


def per_device(tokens, cotangent, route_gates, routes, w_gate, w_up, w_down):
    experts, group = lax.axis_size("expert"), lax.axis_size("dp")
    blocks = experts * group
    token_count, top_count = routes.shape
    width = tokens.shape[1]
    capacity = max(2, token_count * top_count * 4 // (3 * experts))
    total, slots, sent = blocks * token_count, blocks * capacity, experts * capacity
    gate_shard, up_shard, down_shard = (w_gate[0], w_up[0], w_down[0])
    me = lax.axis_index("expert")

    routing = jnp.concatenate([routes.astype(jnp.bfloat16), route_gates], axis=1)
    routing = jnp.pad(routing, ((0, 0), (0, 128 - 2 * top_count)))
    routing, all_tokens, all_cot = gather_all(experts, group, [routing, tokens, cotangent])
    routing = routing[:, : 2 * top_count].astype(jnp.float32)

    match = (routing[:, :top_count] == me.astype(jnp.float32)).astype(jnp.float32)
    gates = jnp.sum(match * routing[:, top_count:], axis=1)
    used = jnp.sum(match, axis=1).reshape(blocks, token_count)
    order = jnp.arange(token_count, dtype=jnp.int32)
    lower = (order[:, None] < order[None, :]).astype(jnp.bfloat16)
    rank = dot_f32(used.astype(jnp.bfloat16), lower)
    number = jnp.arange(blocks, dtype=jnp.int32)
    base = ((number % group) * experts + number // group) * capacity
    slot = jnp.where(used > 0, rank + base.astype(jnp.float32)[:, None], -1.0).reshape(total)
    slot_ids = jnp.arange(slots, dtype=jnp.int32).astype(jnp.float32)
    hit = slot_ids[:, None] == slot[None, :]
    pick = hit.astype(jnp.bfloat16)
    row_gate = jnp.sum(jnp.where(hit, gates[None, :], 0.0), axis=1)

    expert_ids = jnp.arange(experts, dtype=jnp.int32)
    named = routes[:, :, None] == expert_ids[None, None, :]
    mine = jnp.sum(named.astype(jnp.int32), axis=1)
    place = jnp.cumsum(mine, axis=0) - mine + expert_ids[None, :] * capacity
    route_slot = jnp.sum(jnp.where(named, place[:, None, :], 0), axis=2)
    taken = route_slot[:, :, None] == jnp.arange(sent, dtype=jnp.int32)[None, None, :]
    token_table = jnp.sum(taken.astype(jnp.float32), axis=1).astype(jnp.bfloat16)
    gate_table = jnp.sum(
        jnp.where(taken, route_gates.astype(jnp.float32)[:, :, None], 0.0), axis=1
    ).astype(jnp.bfloat16)
    own_cot = dot_f32(token_table, cotangent, OUTER)

    def send_home(part):
        part = lax.psum_scatter(
            part.reshape(group, sent, width), "dp", scatter_dimension=0, tiled=True
        )
        part = part.reshape(experts, capacity, width)
        part = lax.all_to_all(part, "expert", split_axis=0, concat_axis=0, tiled=True)
        return part.reshape(sent, width)

    rows_in = dot_f32(pick, all_tokens).astype(jnp.bfloat16)
    gate_pre = dot_f32(rows_in, gate_shard, INNER)
    up_pre = dot_f32(rows_in, up_shard, INNER)
    sig = jax.nn.sigmoid(gate_pre)
    hidden = (gate_pre * sig * up_pre).astype(jnp.bfloat16)
    back_out = send_home(dot_f32(hidden, down_shard).astype(jnp.bfloat16))
    rows_back = (dot_f32(pick, all_cot) * row_gate[:, None]).astype(jnp.bfloat16)
    back_hidden = dot_f32(rows_back, down_shard, INNER)
    grad_pre = (back_hidden * up_pre * sig * (1.0 + gate_pre * (1.0 - sig))).astype(jnp.bfloat16)
    grad_upv = (back_hidden * gate_pre * sig).astype(jnp.bfloat16)
    back_part = (dot_f32(grad_pre, gate_shard) + dot_f32(grad_upv, up_shard)).astype(jnp.bfloat16)
    back_grad = send_home(back_part)
    grad_down = dot_f32(hidden, rows_back, OUTER)
    grad_gate = dot_f32(grad_pre, rows_in, OUTER)
    grad_up = dot_f32(grad_upv, rows_in, OUTER)

    mixed = dot_f32(gate_table, back_out).astype(jnp.bfloat16)
    token_grad = dot_f32(token_table, back_grad).astype(jnp.bfloat16)
    row_grad = jnp.sum(own_cot * back_out.astype(jnp.float32), axis=1)
    gate_grad = jnp.sum(jnp.where(taken, row_grad[None, None, :], 0.0), axis=2)
    return (mixed, token_grad, gate_grad, grad_gate[None], grad_up[None], grad_down[None])


def solution(mesh):
    row = P(("expert", "dp"), None)
    wide = P("expert", "dp", None)
    return jax.shard_map(
        per_device,
        mesh=mesh,
        in_specs=(row, row, row, row, wide, wide, wide),
        out_specs=(row, row, row, wide, wide, wide),
        check_vma=False,
    )
```

time: 354 us -> 159 us (0.45)
  waiting for transfers between devices: 213 us -> 29.4 us
  blocking collectives: 75.9 us -> 0 us
  Pallas kernels: 0 us -> 46.9 us
  starting transfers between devices: 0.34 us -> 12.1 us
  local copies, waits for them, and re-layouts: 3.19 us -> 11.3 us
  matrix products: 44.1 us -> 39.9 us
    reduce_scatter x2, waiting for transfers between devices: 143 us -> 6.17 us  [send_home(): lax.psum_scatter(part.reshape(group, sent, width), 'dp', scatter_dimensio...]
    all_gather x2 -> x0, waiting for transfers between devices: 68.6 us -> none  [the longest x1 45.9 us: per_device(): all_cot = lax.all_gather(cotangent, AXES, axis=0, tiled=True)]
    pallas_call x0 -> x1, Pallas kernels: none -> 46.9 us  [gather_all(): pl.pallas_call(functools.partial(gather_kernel, depth, group), out_shape=...]
    unnamed x1 -> x0, blocking collectives: 39.6 us -> none
    all_gather x1 -> x0, blocking collectives: 36.3 us -> none  [per_device(): routing = lax.all_gather(routing, AXES, axis=0, tiled=True)]
    all_to_all x0 -> x2, waiting for transfers between devices: none -> 23.2 us  [send_home(): lax.all_to_all(part, 'expert', split_axis=0, concat_axis=0, tiled=True)]
    all_to_all x0 -> x2, starting transfers between devices: none -> 12.1 us  [send_home(): lax.all_to_all(part, 'expert', split_axis=0, concat_axis=0, tiled=True)]
    reshape x0 -> x4, local copies, waits for them, and re-layouts: none -> 8.45 us  [the longest x2 4.25 us: send_home(): part = part.reshape(experts, capacity, width)]
  transfers between devices with their start and end apart: 4 -> 4, of which waited for: 4 -> 4; matrix products, arithmetic and copies ran while one was open for 13% -> 20% of each run, Pallas kernels for 0% -> 0%
where the time goes in v2:
time: 159 us; the launch traced here: 158 us
  Pallas kernels  46.9 us (29%)
  matrix products  39.9 us (25%)
  waiting for transfers between devices  29.4 us (18%)
  between operations  14.3 us (9%)
  starting transfers between devices  12.1 us (8%)
  local copies, waits for them, and re-layouts  11.3 us (7%)
  other arithmetic  4.07 us (3%)
    pallas_call x1, Pallas kernels, gather_all(): pl.pallas_call(functools.partial(gather_kernel, depth, group), out_shape=...  46.9 us
    dot_general x15, matrix products, dot_f32(): lax.dot_general(left, right, dims, preferred_element_type=jnp.float32)  39.9 us
    all_to_all x2, waiting for transfers between devices, send_home(): lax.all_to_all(part, 'expert', split_axis=0, concat_axis=0, tiled=True)  23.2 us
    all_to_all x2, starting transfers between devices, send_home(): lax.all_to_all(part, 'expert', split_axis=0, concat_axis=0, tiled=True)  12.1 us
    reduce_scatter x2, waiting for transfers between devices, send_home(): lax.psum_scatter(part.reshape(group, sent, width), 'dp', scatter_dimensio...  6.17 us
    reshape x2, local copies, waits for them, and re-layouts, send_home(): part = part.reshape(experts, capacity, width)  4.25 us
    reshape x2, local copies, waits for them, and re-layouts, send_home(): return part.reshape(sent, width)  4.2 us
  transfers between devices with their start and end apart: 4, of which 4 were waited for; matrix products, arithmetic and copies ran while one was open for 20% of the time, Pallas kernels for 0%

profile of v2, /device:TPU:8, one launch (start us, length us, event | category | flops | bytes accessed | tf_op | source)
XLA Modules:
  0.0 158.0 jit_solution(12597669473278888500)
XLA Ops:
  9.7 46.9 %shard_map.118 = (bf16[4,2,2,2,24,128]{5,4,3,2,1,0:T(8,128)(2,1)}, bf16[4,2,2,2,24,2048]{5,4,3,2,1,0:T(8,128)(2,1)}, bf16[4,2,2,2,24,2048]{5,4,3,2,1,0:T(8,128)(2,1)}) custom-call(bf16[24,128]{1,0:T(8,128)(2,1)} %fusion.30.refs_0_, bf16[24,2048]{1,0:T(8,128)(2,1)} %refs_1_.1, bf16[24,2048]{1,0:T(8,128)(2,1)} %refs_2_.1), custom_call_target="tpu_custom_call" | custom-call | tf_op jit(solution)/shard_map/pallas_call | solution.py:135
  58.6 3.5 %convolution_convert_fusion = bf16[384,2048]{1,0:T(8,128)(2,1)S(1)} fusion(bf16[768,2048]{1,0:T(8,128)(2,1)} %bitcast.57, f32[768]{0:T(1024)S(1)} %eq.58, f32[384]{0:T(512)S(1)} %iota_convert_fusion), kind=kOutput, calls=%fused_computation.18 | convolution fusion | flops 1209040896 | bytes 4723200 | tf_op jit(solution)/shard_map/dot_general | solution.py:15
  64.5 1.7 %fusion = f32[384,704]{0,1:T(8,128)S(1)} fusion(bf16[384,2048]{1,0:T(8,128)(2,1)S(1)} %multiply_convert_fusion, bf16[1,704,2048]{2,1,0:T(8,128)(2,1)S(1)} %copy-done.4), kind=kOutput, calls=%fused_computation.5 | convolution fusion | flops 1107296256 | bytes 5537792 | tf_op jit(solution)/shard_map/dot_general | solution.py:15
  66.8 1.7 %fusion.6 = f32[384,704]{0,1:T(8,128)S(1)} fusion(bf16[384,2048]{1,0:T(8,128)(2,1)S(1)} %convolution_convert_fusion, bf16[1,704,2048]{2,1,0:T(8,128)(2,1)S(1)} %copy-done.1), kind=kOutput, calls=%fused_computation.11 | convolution fusion | flops 1107296256 | bytes 5537792 | tf_op jit(solution)/shard_map/dot_general | solution.py:15
  68.6 2.9 %multiply_convert_fusion.2 = (bf16[384,704]{0,1:T(8,128)(2,1)}, bf16[384,704]{0,1:T(8,128)(2,1)S(1)}, bf16[384,704]{0,1:T(8,128)(2,1)S(1)}) fusion(f32[384,704]{0,1:T(8,128)S(1)} %fusion, f32[384,704]{0,1:T(8,128)S(1)} %fusion.6, bf16[384,2048]{1,0:T(8,128)(2,1)S(1)} %convolution_convert_fusion, bf16[1,704,2048]{2,1,0:T(8,128)(2,1)S(1)} %copy-done), kind=kOutput, calls=%fused_computation.30 | convolution fusion | flops 1111621632 | bytes 8241152 | tf_op jit(solution)/shard_map/dot_general | solution.py:15
  71.5 2.6 %fusion.12 = bf16[384,2048]{1,0:T(8,128)(2,1)} fusion(bf16[384,704]{0,1:T(8,128)(2,1)S(1)} %get-tuple-element.17, bf16[1,704,2048]{2,1,0:T(8,128)(2,1)S(1)} %copy-done.4), kind=kOutput, calls=%fused_computation.17 | convolution fusion | flops 1108082688 | bytes 4997120 | tf_op jit(solution)/shard_map/dot_general | solution.py:15
  74.1 3.3 %fusion.4 = f32[384,2048]{1,0:T(8,128)S(1)} fusion(bf16[384,704]{0,1:T(8,128)(2,1)S(1)} %get-tuple-element.18, bf16[1,704,2048]{2,1,0:T(8,128)(2,1)} %param.12), kind=kOutput, calls=%fused_computation.9 | convolution fusion | flops 1107296256 | bytes 6569984 | tf_op jit(solution)/shard_map/dot_general | solution.py:15
  77.4 2.7 %add_convert_fusion = bf16[384,2048]{1,0:T(8,128)(2,1)} fusion(f32[384,2048]{1,0:T(8,128)S(1)} %fusion.4, bf16[384,704]{0,1:T(8,128)(2,1)S(1)} %copy-done.5, bf16[1,704,2048]{2,1,0:T(8,128)(2,1)S(1)} %copy-done), kind=kOutput, calls=%fused_computation.3 | convolution fusion | flops 1108869120 | bytes 8142848 | tf_op jit(solution)/shard_map/dot_general | solution.py:15
  80.1 2.4 %reduce-scatter.3.cloned.1.call-done = bf16[1,192,2048]{2,1,0:T(8,128)(2,1)} async-done(((bf16[2,192,2048]{2,1,0:T(8,128)(2,1)}), bf16[1,192,2048]{2,1,0:T(8,128)(2,1)}) %reduce-scatter.3.cloned.1.call-update) | async-done | bytes 786448 | tf_op jit(solution)/shard_map/reduce_scatter | solution.py:192
  82.5 2.1 %reshape.107 = bf16[16,12,2048]{2,1,0:T(8,128)(2,1)} reshape(bf16[1,192,2048]{2,1,0:T(8,128)(2,1)} %reduce-scatter.3.cloned.1.call-done) | data formatting | bytes 1572864 | tf_op jit(solution)/shard_map/reshape | solution.py:195
  84.6 7.0 %all-to-all-start = ((bf16[16,12,2048]{2,1,0:T(8,128)(2,1)}), bf16[16,12,2048]{2,1,0:T(8,128)(2,1)}, u32[]{:S(2)}, u32[]{:S(2)}) async-start(bf16[16,12,2048]{2,1,0:T(8,128)(2,1)} %reshape.107), calls=%async_computation.1 | async-start | bytes 2097152 | tf_op jit(solution)/shard_map/all_to_all | solution.py:196
  91.8 3.8 %reduce-scatter.5.cloned.1.call-done = bf16[1,192,2048]{2,1,0:T(8,128)(2,1)} async-done(((bf16[2,192,2048]{2,1,0:T(8,128)(2,1)}), bf16[1,192,2048]{2,1,0:T(8,128)(2,1)}) %reduce-scatter.5.cloned.1.call-update) | async-done | bytes 786448 | tf_op jit(solution)/shard_map/reduce_scatter | solution.py:192
  95.6 2.1 %reshape.111 = bf16[16,12,2048]{2,1,0:T(8,128)(2,1)} reshape(bf16[1,192,2048]{2,1,0:T(8,128)(2,1)} %reduce-scatter.5.cloned.1.call-done) | data formatting | bytes 1572864 | tf_op jit(solution)/shard_map/reshape | solution.py:195
  97.8 19.6 %all-to-all-done = bf16[16,12,2048]{2,1,0:T(8,128)(2,1)} async-done(((bf16[16,12,2048]{2,1,0:T(8,128)(2,1)}), bf16[16,12,2048]{2,1,0:T(8,128)(2,1)}, u32[]{:S(2)}, u32[]{:S(2)}) %all-to-all-start) | async-done | bytes 786464 | tf_op jit(solution)/shard_map/all_to_all | solution.py:196
  117.4 5.1 %all-to-all-start.1 = ((bf16[16,12,2048]{2,1,0:T(8,128)(2,1)}), bf16[16,12,2048]{2,1,0:T(8,128)(2,1)}, u32[]{:S(2)}, u32[]{:S(2)}) async-start(bf16[16,12,2048]{2,1,0:T(8,128)(2,1)} %reshape.111), calls=%async_computation.3 | async-start | bytes 2097152 | tf_op jit(solution)/shard_map/all_to_all | solution.py:196
  122.7 5.9 %convolution_bitcast_fusion = f32[1,704,2048]{2,1,0:T(8,128)} fusion(bf16[384,704]{0,1:T(8,128)(2,1)} %copy-done.7, bf16[384,2048]{1,0:T(8,128)(2,1)} %copy-done.8), kind=kOutput, calls=%fused_computation | convolution fusion | flops 1107296256 | bytes 7880704 | tf_op jit(solution)/shard_map/dot_general | solution.py:15
  128.6 4.2 %convolution_bitcast_fusion.2 = f32[1,704,2048]{2,1,0:T(8,128)} fusion(bf16[384,704]{0,1:T(8,128)(2,1)S(1)} %copy-done.6, bf16[384,2048]{1,0:T(8,128)(2,1)S(1)} %copy-done.3), kind=kOutput, calls=%fused_computation.2 | convolution fusion | flops 1107296256 | bytes 7880704 | tf_op jit(solution)/shard_map/dot_general | solution.py:15
  132.8 4.2 %convolution_bitcast_fusion.1 = f32[1,704,2048]{2,1,0:T(8,128)} fusion(bf16[384,704]{0,1:T(8,128)(2,1)S(1)} %get-tuple-element.18, bf16[384,2048]{1,0:T(8,128)(2,1)S(1)} %copy-done.3), kind=kOutput, calls=%fused_computation.1 | convolution fusion | flops 1107296256 | bytes 7880704 | tf_op jit(solution)/shard_map/dot_general | solution.py:15
  137.0 2.1 %reshape.108 = bf16[192,2048]{1,0:T(8,128)(2,1)} reshape(bf16[16,12,2048]{2,1,0:T(8,128)(2,1)} %all-to-all-done) | data formatting | bytes 1572864 | tf_op jit(solution)/shard_map/reshape | solution.py:197
  139.1 1.6 %fusion.19 = f32[192]{0:T(256)S(1)} fusion(bf16[192,2048]{1,0:T(8,128)(2,1)} %reshape.108, bf16[24,2048]{1,0:T(8,128)(2,1)S(1)} %copy-done.9, bf16[24,192]{1,0:T(8,128)(2,1)S(1)} %convert_reduce_fusion.1), kind=kOutput, calls=%fused_computation.25 | convolution fusion | flops 20053824 | bytes 894720 | tf_op jit(solution)/shard_map/dot_general | solution.py:15
  141.5 2.0 %convolution_convert_fusion.2 = bf16[24,2048]{1,0:T(8,128)(2,1)} fusion(bf16[192,2048]{1,0:T(8,128)(2,1)} %reshape.108, bf16[24,192]{1,0:T(8,128)(2,1)S(1)} %get-tuple-element.15), kind=kOutput, calls=%fused_computation.21 | convolution fusion | flops 18923520 | bytes 893952 | tf_op jit(solution)/shard_map/dot_general | solution.py:15
  143.5 3.6 %all-to-all-done.1 = bf16[16,12,2048]{2,1,0:T(8,128)(2,1)} async-done(((bf16[16,12,2048]{2,1,0:T(8,128)(2,1)}), bf16[16,12,2048]{2,1,0:T(8,128)(2,1)}, u32[]{:S(2)}, u32[]{:S(2)}) %all-to-all-start.1) | async-done | bytes 786464 | tf_op jit(solution)/shard_map/all_to_all | solution.py:196
  147.1 2.1 %reshape.112 = bf16[192,2048]{1,0:T(8,128)(2,1)} reshape(bf16[16,12,2048]{2,1,0:T(8,128)(2,1)} %all-to-all-done.1) | data formatting | bytes 1572864 | tf_op jit(solution)/shard_map/reshape | solution.py:197
  149.2 2.0 %convolution_convert_fusion.1 = bf16[24,2048]{1,0:T(8,128)(2,1)} fusion(bf16[192,2048]{1,0:T(8,128)(2,1)} %reshape.112, bf16[24,192]{1,0:T(8,128)(2,1)S(1)} %convert_reduce_fusion.1), kind=kOutput, calls=%fused_computation.20 | convolution fusion | flops 18923520 | bytes 893952 | tf_op jit(solution)/shard_map/dot_general | solution.py:15
  (58 shorter events, 8.7 us)
Async XLA Ops:
  7.2 61.4 %copy-start = (bf16[1,704,2048]{2,1,0:T(8,128)(2,1)S(1)}, bf16[1,704,2048]{2,1,0:T(8,128)(2,1)}, u32[]{:S(2)}) copy-start(bf16[1,704,2048]{2,1,0:T(8,128)(2,1)} %param.11) | copy-start | bytes 8650756
  7.2 75.3 %reduce-scatter.3.cloned.1.call-start = ((), (), s32[]{:S(2)}) async-start(), calls=%async_computation.4 | async-start | bytes 2359296 | tf_op jit(solution)/shard_map/reduce_scatter | solution.py:192
  58.6 3.8 %copy-start.12 = (bf16[4,2,2,2,24,2048]{5,4,3,2,1,0:T(8,128)(2,1)S(1)}, bf16[4,2,2,2,24,2048]{5,4,3,2,1,0:T(8,128)(2,1)}, u32[]{:S(2)}) copy-start(bf16[4,2,2,2,24,2048]{5,4,3,2,1,0:T(8,128)(2,1)} %get-tuple-element.11) | copy-start | bytes 9437188
  62.1 6.5 %copy-start.2 = (bf16[384,2048]{1,0:T(8,128)(2,1)}, bf16[384,2048]{1,0:T(8,128)(2,1)S(1)}, u32[]{:S(2)}) copy-start(bf16[384,2048]{1,0:T(8,128)(2,1)S(1)} %convolution_convert_fusion) | copy-start | bytes 4718596
  62.4 2.1 %copy-start.4 = (bf16[1,704,2048]{2,1,0:T(8,128)(2,1)S(1)}, bf16[1,704,2048]{2,1,0:T(8,128)(2,1)}, u32[]{:S(2)}) copy-start(bf16[1,704,2048]{2,1,0:T(8,128)(2,1)} %param.13) | copy-start | bytes 8650756
  64.5 1.7 %copy-start.8 = (bf16[384,2048]{1,0:T(8,128)(2,1)}, bf16[384,2048]{1,0:T(8,128)(2,1)S(1)}, u32[]{:S(2)}) copy-start(bf16[384,2048]{1,0:T(8,128)(2,1)S(1)} %multiply_convert_fusion) | copy-start | bytes 4718596
  64.5 2.4 %copy-start.1 = (bf16[1,704,2048]{2,1,0:T(8,128)(2,1)S(1)}, bf16[1,704,2048]{2,1,0:T(8,128)(2,1)}, u32[]{:S(2)}) copy-start(bf16[1,704,2048]{2,1,0:T(8,128)(2,1)} %param.12) | copy-start | bytes 8650756
  71.5 2.6 %copy-start.7 = (bf16[384,704]{0,1:T(8,128)(2,1)}, bf16[384,704]{0,1:T(8,128)(2,1)S(1)}, u32[]{:S(2)}) copy-start(bf16[384,704]{0,1:T(8,128)(2,1)S(1)} %get-tuple-element.17) | copy-start | bytes 1622020
  74.1 21.6 %reduce-scatter.5.cloned.1.call-start = ((), (), s32[]{:S(2)}) async-start(), calls=%async_computation.5 | async-start | bytes 2359296 | tf_op jit(solution)/shard_map/reduce_scatter | solution.py:192
  74.1 3.3 %copy-start.5 = (bf16[384,704]{0,1:T(8,128)(2,1)S(1)}, bf16[384,704]{0,1:T(8,128)(2,1)}, u32[]{:S(2)}) copy-start(bf16[384,704]{0,1:T(8,128)(2,1)} %get-tuple-element.16) | copy-start | bytes 1622020
  80.1 11.4 %copy-start.10 = (s32[24,6]{0,1:T(8,128)S(1)}, s32[24,6]{0,1:T(8,128)}, u32[]{:S(2)}) copy-start(s32[24,6]{0,1:T(8,128)} %param.10) | copy-start | bytes 1732
  84.6 32.8 %all-to-all-start = ((bf16[16,12,2048]{2,1,0:T(8,128)(2,1)}), bf16[16,12,2048]{2,1,0:T(8,128)(2,1)}, u32[]{:S(2)}, u32[]{:S(2)}) async-start(bf16[16,12,2048]{2,1,0:T(8,128)(2,1)} %reshape.107), calls=%async_computation.1 | async-start | bytes 2097152 | tf_op jit(solution)/shard_map/all_to_all | solution.py:196
  91.8 30.8 %copy-start.11 = (bf16[24,6]{0,1:T(8,128)(2,1)S(1)}, bf16[24,6]{0,1:T(8,128)(2,1)}, u32[]{:S(2)}) copy-start(bf16[24,6]{0,1:T(8,128)(2,1)} %param.9) | copy-start | bytes 868
  117.4 29.7 %all-to-all-start.1 = ((bf16[16,12,2048]{2,1,0:T(8,128)(2,1)}), bf16[16,12,2048]{2,1,0:T(8,128)(2,1)}, u32[]{:S(2)}, u32[]{:S(2)}) async-start(bf16[16,12,2048]{2,1,0:T(8,128)(2,1)} %reshape.111), calls=%async_computation.3 | async-start | bytes 2097152 | tf_op jit(solution)/shard_map/all_to_all | solution.py:196
  122.6 5.9 %copy-start.3 = (bf16[384,2048]{1,0:T(8,128)(2,1)S(1)}, bf16[384,2048]{1,0:T(8,128)(2,1)}, u32[]{:S(2)}) copy-start(bf16[384,2048]{1,0:T(8,128)(2,1)} %copy-done.2) | copy-start | bytes 4718596
  122.7 5.9 %copy-start.6 = (bf16[384,704]{0,1:T(8,128)(2,1)S(1)}, bf16[384,704]{0,1:T(8,128)(2,1)}, u32[]{:S(2)}) copy-start(bf16[384,704]{0,1:T(8,128)(2,1)} %get-tuple-element.16) | copy-start | bytes 1622020
  137.0 2.1 %copy-start.9 = (bf16[24,2048]{1,0:T(8,128)(2,1)S(1)}, bf16[24,2048]{1,0:T(8,128)(2,1)}, u32[]{:S(2)}) copy-start(bf16[24,2048]{1,0:T(8,128)(2,1)} %refs_2_.1) | copy-start | bytes 294916
Sparse Core Ops, SparseCore 0:
  74.2 8.2 reduce-scatter.2
  85.3 10.2 reduce-scatter.4

commit v3 on v2

--- a/solution.py
+++ b/solution.py
@@ -6,6 +6,7 @@
 from jax.experimental import pallas as pl
 from jax.experimental.pallas import tpu as pltpu
 from jax.sharding import PartitionSpec as P
+
 
 INNER = (((1,), (1,)), ((), ()))
 OUTER = (((0,), (0,)), ((), ()))
@@ -188,10 +189,11 @@
     ).astype(jnp.bfloat16)
     own_cot = dot_f32(token_table, cotangent, OUTER)
 
+    def sum_halves(part):
+        part = part.reshape(group, sent, width)
+        return lax.psum_scatter(part, "dp", scatter_dimension=0, tiled=True)
+
     def send_home(part):
-        part = lax.psum_scatter(
-            part.reshape(group, sent, width), "dp", scatter_dimension=0, tiled=True
-        )
         part = part.reshape(experts, capacity, width)
         part = lax.all_to_all(part, "expert", split_axis=0, concat_axis=0, tiled=True)
         return part.reshape(sent, width)
@@ -201,13 +203,17 @@
     up_pre = dot_f32(rows_in, up_shard, INNER)
     sig = jax.nn.sigmoid(gate_pre)
     hidden = (gate_pre * sig * up_pre).astype(jnp.bfloat16)
-    back_out = send_home(dot_f32(hidden, down_shard).astype(jnp.bfloat16))
+    out_part = dot_f32(hidden, down_shard).astype(jnp.bfloat16)
+    out_part, all_cot = lax.optimization_barrier((out_part, all_cot))
+    out_sum = sum_halves(out_part)
     rows_back = (dot_f32(pick, all_cot) * row_gate[:, None]).astype(jnp.bfloat16)
     back_hidden = dot_f32(rows_back, down_shard, INNER)
     grad_pre = (back_hidden * up_pre * sig * (1.0 + gate_pre * (1.0 - sig))).astype(jnp.bfloat16)
     grad_upv = (back_hidden * gate_pre * sig).astype(jnp.bfloat16)
+    out_sum, grad_pre, grad_upv = lax.optimization_barrier((out_sum, grad_pre, grad_upv))
+    back_out = send_home(out_sum)
     back_part = (dot_f32(grad_pre, gate_shard) + dot_f32(grad_upv, up_shard)).astype(jnp.bfloat16)
-    back_grad = send_home(back_part)
+    back_grad = send_home(sum_halves(back_part))
     grad_down = dot_f32(hidden, rows_back, OUTER)
     grad_gate = dot_f32(grad_pre, rows_in, OUTER)
     grad_up = dot_f32(grad_upv, rows_in, OUTER)

time: 159 us -> 160 us (level)
  matrix products: 39.9 us -> 42.8 us
    reduce_scatter x2, waiting for transfers between devices: 6.17 us -> 1.77 us  [sum_halves(): return lax.psum_scatter(part, 'dp', scatter_dimension=0, tiled=True)]
    dot_general x15, matrix products: 39.9 us -> 42.8 us  [dot_f32(): lax.dot_general(left, right, dims, preferred_element_type=jnp.float32)]
    all_to_all x2, waiting for transfers between devices: 23.2 us -> 26 us  [send_home(): lax.all_to_all(part, 'expert', split_axis=0, concat_axis=0, tiled=True)]
where the time goes in v3:
time: 160 us
  Pallas kernels  46.9 us (29%)
  matrix products  42.8 us (27%)
  waiting for transfers between devices  27.8 us (17%)
  between operations  14.3 us (9%)
  starting transfers between devices  12.1 us (8%)
  local copies, waits for them, and re-layouts  11.8 us (7%)
  other arithmetic  4.07 us (3%)
    pallas_call x1, Pallas kernels, gather_all(): pl.pallas_call(functools.partial(gather_kernel, depth, group), out_shape=...  46.9 us
    dot_general x15, matrix products, dot_f32(): lax.dot_general(left, right, dims, preferred_element_type=jnp.float32)  42.8 us
    all_to_all x2, waiting for transfers between devices, send_home(): lax.all_to_all(part, 'expert', split_axis=0, concat_axis=0, tiled=True)  26 us
    all_to_all x2, starting transfers between devices, send_home(): lax.all_to_all(part, 'expert', split_axis=0, concat_axis=0, tiled=True)  12 us
    reshape x2, local copies, waits for them, and re-layouts, send_home(): part = part.reshape(experts, capacity, width)  4.28 us
    reshape x2, local copies, waits for them, and re-layouts, send_home(): return part.reshape(sent, width)  4.2 us
  transfers between devices with their start and end apart: 4, of which 4 were waited for; matrix products, arithmetic and copies ran while one was open for 20% of the time, Pallas kernels for 0%

profile of v3, /device:TPU:8, one launch (start us, length us, event | category | flops | bytes accessed | tf_op | source)
XLA Modules:
  0.0 159.8 jit_solution(826964524223860965)
XLA Ops:
  9.7 46.9 %shard_map.118 = (bf16[4,2,2,2,24,128]{5,4,3,2,1,0:T(8,128)(2,1)}, bf16[4,2,2,2,24,2048]{5,4,3,2,1,0:T(8,128)(2,1)}, bf16[4,2,2,2,24,2048]{5,4,3,2,1,0:T(8,128)(2,1)}) custom-call(bf16[24,128]{1,0:T(8,128)(2,1)} %fusion.30.refs_0_, bf16[24,2048]{1,0:T(8,128)(2,1)} %refs_1_.1, bf16[24,2048]{1,0:T(8,128)(2,1)} %refs_2_.1), custom_call_target="tpu_custom_call" | custom-call | tf_op jit(solution)/shard_map/pallas_call | solution.py:136
  58.6 3.5 %convolution_convert_fusion = bf16[384,2048]{1,0:T(8,128)(2,1)S(1)} fusion(bf16[768,2048]{1,0:T(8,128)(2,1)} %bitcast.59, f32[768]{0:T(1024)S(1)} %eq.58, f32[384]{0:T(512)S(1)} %iota_convert_fusion), kind=kOutput, calls=%fused_computation.18 | convolution fusion | flops 1209040896 | bytes 4723200 | tf_op jit(solution)/shard_map/dot_general | solution.py:16
  62.1 1.7 %fusion.10 = f32[384,704]{0,1:T(8,128)S(1)} fusion(bf16[384,2048]{1,0:T(8,128)(2,1)S(1)} %convolution_convert_fusion, bf16[1,704,2048]{2,1,0:T(8,128)(2,1)S(1)} %copy-done.4), kind=kOutput, calls=%fused_computation.15 | convolution fusion | flops 1107296256 | bytes 5537792 | tf_op jit(solution)/shard_map/dot_general | solution.py:16
  64.5 2.7 %multiply_convert_fusion.3 = (bf16[384,704]{0,1:T(8,128)(2,1)S(1)}, f32[384,704]{0,1:T(8,128)}) fusion(f32[384,704]{0,1:T(8,128)S(1)} %fusion.10, bf16[384,2048]{1,0:T(8,128)(2,1)S(1)} %convolution_convert_fusion, bf16[1,704,2048]{2,1,0:T(8,128)(2,1)S(1)} %copy-done.1), kind=kOutput, calls=%fused_computation.31 | convolution fusion | flops 1108918272 | bytes 7159808 | tf_op jit(solution)/shard_map/dot_general | solution.py:16
  67.2 2.6 %fusion.12 = bf16[384,2048]{1,0:T(8,128)(2,1)} fusion(bf16[384,704]{0,1:T(8,128)(2,1)S(1)} %get-tuple-element.28, bf16[1,704,2048]{2,1,0:T(8,128)(2,1)S(1)} %copy-done), kind=kOutput, calls=%fused_computation.17 | convolution fusion | flops 1108082688 | bytes 4997120 | tf_op jit(solution)/shard_map/dot_general | solution.py:16
  70.1 3.5 %multiply_convert_fusion = bf16[384,2048]{1,0:T(8,128)(2,1)S(1)} fusion(bf16[768,2048]{1,0:T(8,128)(2,1)} %bitcast.58, f32[384]{0:T(512)S(1)} %fusion.20, f32[768]{0:T(1024)S(1)} %eq.58, f32[384]{0:T(512)S(1)} %iota_convert_fusion), kind=kOutput, calls=%fused_computation.4 | convolution fusion | flops 1209827328 | bytes 4724736 | tf_op jit(solution)/shard_map/dot_general | solution.py:16
  73.6 1.1 copy-done.9
  74.7 2.8 %multiply_convert_fusion.1 = (bf16[384,704]{0,1:T(8,128)(2,1)S(1)}, bf16[384,704]{0,1:T(8,128)(2,1)}) fusion(f32[384,704]{0,1:T(8,128)S(1)} %copy-done.14, f32[384,704]{0,1:T(8,128)S(1)} %copy-done.15, bf16[384,2048]{1,0:T(8,128)(2,1)S(1)} %multiply_convert_fusion, bf16[1,704,2048]{2,1,0:T(8,128)(2,1)S(1)} %copy-done), kind=kOutput, calls=%fused_computation.29 | convolution fusion | flops 1110810624 | bytes 7700480 | tf_op jit(solution)/shard_map/dot_general | solution.py:16
  78.2 3.4 %fusion.4 = f32[384,2048]{1,0:T(8,128)S(1)} fusion(bf16[384,704]{0,1:T(8,128)(2,1)S(1)} %get-tuple-element.21, bf16[1,704,2048]{2,1,0:T(8,128)(2,1)} %param.12), kind=kOutput, calls=%fused_computation.9 | convolution fusion | flops 1107296256 | bytes 6569984 | tf_op jit(solution)/shard_map/dot_general | solution.py:16
  81.6 2.7 %add_convert_fusion = bf16[384,2048]{1,0:T(8,128)(2,1)} fusion(f32[384,2048]{1,0:T(8,128)S(1)} %fusion.4, bf16[384,704]{0,1:T(8,128)(2,1)S(1)} %copy-done.7, bf16[1,704,2048]{2,1,0:T(8,128)(2,1)S(1)} %copy-done.5), kind=kOutput, calls=%fused_computation.3 | convolution fusion | flops 1108869120 | bytes 8142848 | tf_op jit(solution)/shard_map/dot_general | solution.py:16
  84.3 2.1 %reshape.108 = bf16[16,12,2048]{2,1,0:T(8,128)(2,1)} reshape(bf16[1,192,2048]{2,1,0:T(8,128)(2,1)} %reduce-scatter.3.cloned.1.call-done) | data formatting | bytes 1572864 | tf_op jit(solution)/shard_map/reshape | solution.py:197
  86.5 7.0 %all-to-all-start = ((bf16[16,12,2048]{2,1,0:T(8,128)(2,1)}), bf16[16,12,2048]{2,1,0:T(8,128)(2,1)}, u32[]{:S(2)}, u32[]{:S(2)}) async-start(bf16[16,12,2048]{2,1,0:T(8,128)(2,1)} %reshape.108), calls=%async_computation.1 | async-start | bytes 2097152 | tf_op jit(solution)/shard_map/all_to_all | solution.py:198
  94.8 2.1 %reshape.111 = bf16[16,12,2048]{2,1,0:T(8,128)(2,1)} reshape(bf16[1,192,2048]{2,1,0:T(8,128)(2,1)} %reduce-scatter.5.cloned.1.call-done) | data formatting | bytes 1572864 | tf_op jit(solution)/shard_map/reshape | solution.py:197
  96.9 22.4 %all-to-all-done = bf16[16,12,2048]{2,1,0:T(8,128)(2,1)} async-done(((bf16[16,12,2048]{2,1,0:T(8,128)(2,1)}), bf16[16,12,2048]{2,1,0:T(8,128)(2,1)}, u32[]{:S(2)}, u32[]{:S(2)}) %all-to-all-start) | async-done | bytes 786464 | tf_op jit(solution)/shard_map/all_to_all | solution.py:198
  119.3 5.1 %all-to-all-start.1 = ((bf16[16,12,2048]{2,1,0:T(8,128)(2,1)}), bf16[16,12,2048]{2,1,0:T(8,128)(2,1)}, u32[]{:S(2)}, u32[]{:S(2)}) async-start(bf16[16,12,2048]{2,1,0:T(8,128)(2,1)} %reshape.111), calls=%async_computation.3 | async-start | bytes 2097152 | tf_op jit(solution)/shard_map/all_to_all | solution.py:198
  124.5 5.9 %convolution_bitcast_fusion = f32[1,704,2048]{2,1,0:T(8,128)} fusion(bf16[384,704]{0,1:T(8,128)(2,1)} %copy-done.6, bf16[384,2048]{1,0:T(8,128)(2,1)} %copy-done.9), kind=kOutput, calls=%fused_computation | convolution fusion | flops 1107296256 | bytes 7880704 | tf_op jit(solution)/shard_map/dot_general | solution.py:16
  130.4 4.2 %convolution_bitcast_fusion.2 = f32[1,704,2048]{2,1,0:T(8,128)} fusion(bf16[384,704]{0,1:T(8,128)(2,1)S(1)} %copy-done.8, bf16[384,2048]{1,0:T(8,128)(2,1)S(1)} %copy-done.3), kind=kOutput, calls=%fused_computation.2 | convolution fusion | flops 1107296256 | bytes 7880704 | tf_op jit(solution)/shard_map/dot_general | solution.py:16
  134.6 4.2 %convolution_bitcast_fusion.1 = f32[1,704,2048]{2,1,0:T(8,128)} fusion(bf16[384,704]{0,1:T(8,128)(2,1)S(1)} %get-tuple-element.21, bf16[384,2048]{1,0:T(8,128)(2,1)S(1)} %copy-done.3), kind=kOutput, calls=%fused_computation.1 | convolution fusion | flops 1107296256 | bytes 7880704 | tf_op jit(solution)/shard_map/dot_general | solution.py:16
  138.8 2.1 %reshape.109 = bf16[192,2048]{1,0:T(8,128)(2,1)} reshape(bf16[16,12,2048]{2,1,0:T(8,128)(2,1)} %all-to-all-done) | data formatting | bytes 1572864 | tf_op jit(solution)/shard_map/reshape | solution.py:199
  140.9 1.6 %fusion.19 = f32[192]{0:T(256)S(1)} fusion(bf16[192,2048]{1,0:T(8,128)(2,1)} %reshape.109, bf16[24,2048]{1,0:T(8,128)(2,1)S(1)} %copy-done.10, bf16[24,192]{1,0:T(8,128)(2,1)S(1)} %convert_reduce_fusion.1), kind=kOutput, calls=%fused_computation.25 | convolution fusion | flops 20053824 | bytes 894720 | tf_op jit(solution)/shard_map/dot_general | solution.py:16
  143.3 2.0 %convolution_convert_fusion.2 = bf16[24,2048]{1,0:T(8,128)(2,1)} fusion(bf16[192,2048]{1,0:T(8,128)(2,1)} %reshape.109, bf16[24,192]{1,0:T(8,128)(2,1)S(1)} %get-tuple-element.25), kind=kOutput, calls=%fused_computation.21 | convolution fusion | flops 18923520 | bytes 893952 | tf_op jit(solution)/shard_map/dot_general | solution.py:16
  145.3 3.6 %all-to-all-done.1 = bf16[16,12,2048]{2,1,0:T(8,128)(2,1)} async-done(((bf16[16,12,2048]{2,1,0:T(8,128)(2,1)}), bf16[16,12,2048]{2,1,0:T(8,128)(2,1)}, u32[]{:S(2)}, u32[]{:S(2)}) %all-to-all-start.1) | async-done | bytes 786464 | tf_op jit(solution)/shard_map/all_to_all | solution.py:198
  148.9 2.1 %reshape.112 = bf16[192,2048]{1,0:T(8,128)(2,1)} reshape(bf16[16,12,2048]{2,1,0:T(8,128)(2,1)} %all-to-all-done.1) | data formatting | bytes 1572864 | tf_op jit(solution)/shard_map/reshape | solution.py:199
  151.0 2.0 %convolution_convert_fusion.1 = bf16[24,2048]{1,0:T(8,128)(2,1)} fusion(bf16[192,2048]{1,0:T(8,128)(2,1)} %reshape.112, bf16[24,192]{1,0:T(8,128)(2,1)S(1)} %convert_reduce_fusion.1), kind=kOutput, calls=%fused_computation.20 | convolution fusion | flops 18923520 | bytes 893952 | tf_op jit(solution)/shard_map/dot_general | solution.py:16
  (64 shorter events, 8.4 us)
Async XLA Ops:
  7.2 60.0 %copy-start = (bf16[1,704,2048]{2,1,0:T(8,128)(2,1)S(1)}, bf16[1,704,2048]{2,1,0:T(8,128)(2,1)}, u32[]{:S(2)}) copy-start(bf16[1,704,2048]{2,1,0:T(8,128)(2,1)} %param.13) | copy-start | bytes 8650756
  7.2 71.0 %reduce-scatter.3.cloned.1.call-start = ((), (), s32[]{:S(2)}) async-start(), calls=%async_computation.4 | async-start | bytes 2359296 | tf_op jit(solution)/shard_map/reduce_scatter | solution.py:194
  58.6 3.5 %copy-start.4 = (bf16[1,704,2048]{2,1,0:T(8,128)(2,1)S(1)}, bf16[1,704,2048]{2,1,0:T(8,128)(2,1)}, u32[]{:S(2)}) copy-start(bf16[1,704,2048]{2,1,0:T(8,128)(2,1)} %param.11) | copy-start | bytes 8650756
  62.1 1.7 %copy-start.2 = (bf16[384,2048]{1,0:T(8,128)(2,1)}, bf16[384,2048]{1,0:T(8,128)(2,1)S(1)}, u32[]{:S(2)}) copy-start(bf16[384,2048]{1,0:T(8,128)(2,1)S(1)} %convolution_convert_fusion) | copy-start | bytes 4718596
  62.1 2.4 %copy-start.1 = (bf16[1,704,2048]{2,1,0:T(8,128)(2,1)S(1)}, bf16[1,704,2048]{2,1,0:T(8,128)(2,1)}, u32[]{:S(2)}) copy-start(bf16[1,704,2048]{2,1,0:T(8,128)(2,1)} %param.12) | copy-start | bytes 8650756
  64.5 2.7 %copy-start.13 = (f32[384,704]{0,1:T(8,128)}, f32[384,704]{0,1:T(8,128)S(1)}, u32[]{:S(2)}) copy-start(f32[384,704]{0,1:T(8,128)S(1)} %fusion.10) | copy-start | bytes 3244036
  67.2 2.6 %copy-start.6 = (bf16[384,704]{0,1:T(8,128)(2,1)}, bf16[384,704]{0,1:T(8,128)(2,1)S(1)}, u32[]{:S(2)}) copy-start(bf16[384,704]{0,1:T(8,128)(2,1)S(1)} %get-tuple-element.28) | copy-start | bytes 1622020
  69.8 25.0 %reduce-scatter.5.cloned.1.call-start = ((), (), s32[]{:S(2)}) async-start(), calls=%async_computation.5 | async-start | bytes 2359296 | tf_op jit(solution)/shard_map/reduce_scatter | solution.py:194
  70.1 4.6 %copy-start.14 = (f32[384,704]{0,1:T(8,128)S(1)}, f32[384,704]{0,1:T(8,128)}, u32[]{:S(2)}) copy-start(f32[384,704]{0,1:T(8,128)} %copy-done.13) | copy-start | bytes 3244036
  70.1 4.6 %copy-start.15 = (f32[384,704]{0,1:T(8,128)S(1)}, f32[384,704]{0,1:T(8,128)}, u32[]{:S(2)}) copy-start(f32[384,704]{0,1:T(8,128)} %get-tuple-element.29) | copy-start | bytes 3244036
  73.6 1.1 copy-start.9
  78.2 3.4 %copy-start.5 = (bf16[1,704,2048]{2,1,0:T(8,128)(2,1)S(1)}, bf16[1,704,2048]{2,1,0:T(8,128)(2,1)}, u32[]{:S(2)}) copy-start(bf16[1,704,2048]{2,1,0:T(8,128)(2,1)} %param.11) | copy-start | bytes 8650756
  78.2 3.4 %copy-start.7 = (bf16[384,704]{0,1:T(8,128)(2,1)S(1)}, bf16[384,704]{0,1:T(8,128)(2,1)}, u32[]{:S(2)}) copy-start(bf16[384,704]{0,1:T(8,128)(2,1)} %get-tuple-element.20) | copy-start | bytes 1622020
  84.3 9.1 %copy-start.11 = (s32[24,6]{0,1:T(8,128)S(1)}, s32[24,6]{0,1:T(8,128)}, u32[]{:S(2)}) copy-start(s32[24,6]{0,1:T(8,128)} %param.10) | copy-start | bytes 1732
  86.5 32.8 %all-to-all-start = ((bf16[16,12,2048]{2,1,0:T(8,128)(2,1)}), bf16[16,12,2048]{2,1,0:T(8,128)(2,1)}, u32[]{:S(2)}, u32[]{:S(2)}) async-start(bf16[16,12,2048]{2,1,0:T(8,128)(2,1)} %reshape.108), calls=%async_computation.1 | async-start | bytes 2097152 | tf_op jit(solution)/shard_map/all_to_all | solution.py:198
  93.7 30.8 %copy-start.12 = (bf16[24,6]{0,1:T(8,128)(2,1)S(1)}, bf16[24,6]{0,1:T(8,128)(2,1)}, u32[]{:S(2)}) copy-start(bf16[24,6]{0,1:T(8,128)(2,1)} %param.9) | copy-start | bytes 868
  119.3 29.6 %all-to-all-start.1 = ((bf16[16,12,2048]{2,1,0:T(8,128)(2,1)}), bf16[16,12,2048]{2,1,0:T(8,128)(2,1)}, u32[]{:S(2)}, u32[]{:S(2)}) async-start(bf16[16,12,2048]{2,1,0:T(8,128)(2,1)} %reshape.111), calls=%async_computation.3 | async-start | bytes 2097152 | tf_op jit(solution)/shard_map/all_to_all | solution.py:198
  124.5 5.9 %copy-start.3 = (bf16[384,2048]{1,0:T(8,128)(2,1)S(1)}, bf16[384,2048]{1,0:T(8,128)(2,1)}, u32[]{:S(2)}) copy-start(bf16[384,2048]{1,0:T(8,128)(2,1)} %copy-done.2) | copy-start | bytes 4718596
  124.5 5.9 %copy-start.8 = (bf16[384,704]{0,1:T(8,128)(2,1)S(1)}, bf16[384,704]{0,1:T(8,128)(2,1)}, u32[]{:S(2)}) copy-start(bf16[384,704]{0,1:T(8,128)(2,1)} %get-tuple-element.20) | copy-start | bytes 1622020
  138.8 2.1 %copy-start.10 = (bf16[24,2048]{1,0:T(8,128)(2,1)S(1)}, bf16[24,2048]{1,0:T(8,128)(2,1)}, u32[]{:S(2)}) copy-start(bf16[24,2048]{1,0:T(8,128)(2,1)} %refs_2_.1) | copy-start | bytes 294916
Sparse Core Ops, SparseCore 0:
  69.9 8.2 reduce-scatter.2
  84.4 10.2 reduce-scatter.4
